TPU v7x, 128 devices: a whole 4x4x4 slice. The times are simulated.
128 devices in a mesh: tok: 16 (over y, z), head: 8 (over x, core).
Axes of the slice: x: 4, y: 4, z: 4, core: 2. Of those that a mesh axis runs over, the one named last changes fastest.
Arguments:
- hidden_in: bfloat16 [16384, 2048], P('tok', 'head'), may hold values from -6 to 6
- qkv_weight: bfloat16 [2048, 6144], P(None, 'head'), may hold values from -0.125 to 0.125
- dense_weight: bfloat16 [2048, 2048], P('head'), may hold values from -0.125 to 0.125
- up_weight: bfloat16 [2048, 8192], P(None, 'head'), may hold values from -0.125 to 0.125
- down_weight: bfloat16 [8192, 2048], P('head'), may hold values from -0.0625 to 0.0625
- attn_gain: float32 [2048], replicated, may hold values from 0.1 to 1.9
- mlp_gain: float32 [2048], replicated, may hold values from 0.1 to 1.9
- suffix_lengths: int32 [16, 4], replicated, may hold values from 1 to 512, 1024 in all within a row
- request_group: int32 [16, 4], replicated, may hold values from 0 to 15
- prefix_slot: int32 [16], replicated, may hold values from 0 to 15, each once
- prefix_cache: bfloat16 [16, 1024, 4096], P('tok', None, 'head'), may hold values from -204 to 204, as said below
Outputs:
- hidden_out: bfloat16 [16384, 2048], P('tok', 'head')
- suffix_cache: bfloat16 [16384, 4096], P('tok', 'head')
Inputs may be any that keep to these rules, and one draw needn't show every extreme that they name: `suffix_lengths`: each row sums to 1024, and the largest entry of each row is exactly 512. `prefix_slot`: a permutation of the 16 slots. `prefix_cache`: keys already carry rotary embedding at positions 0 to 1023.
All inputs are finite; a program needn't handle non-finite values.
Results may differ from a plain program's by a relative error of at most 0.015.
Values may be sent and summed in bfloat16 or wider, within the bound.
No kernel may reach another device: no remote copies, remote signals or barrier semaphores. Data moves between devices by JAX's collectives and lax.ppermute only.
A program may use at most 192 MiB of HBM per device.

v0:
```python
import functools

import jax
import jax.numpy as jnp
from jax import lax
from jax.experimental import pallas as pl
from jax.experimental.pallas import tpu as pltpu
from jax.sharding import PartitionSpec as P

HD = 256
ROT = 64
D = 2048
FF_DEV = 1024
TOK = 1024
PREFIX = 1024
NC = 2
R = TOK // NC
TILE = 256
STAT = 16
BOTH = ("tok", "head")
F32 = jnp.float32
BF16 = jnp.bfloat16
NEG = -1e30
MIB = 1 << 20
LIMIT_MLP = 18 * MIB
LIMIT_PROJECT = 16 * MIB
LIMIT_OWN = 10 * MIB
LIMIT_PREFIX = 16 * MIB
LIMIT_JOIN = 12 * MIB
LIMIT_REST = 10 * MIB


def flat(y, z, x, c):
    return ((y * 4 + z) * 4 + x) * 2 + c


def permutation(move):
    return [
        (flat(y, z, x, c), flat(*move(y, z, x, c)))
        for y in range(4)
        for z in range(4)
        for x in range(4)
        for c in range(2)
    ]


def permute(value, pairs):
    return lax.ppermute(value, BOTH, pairs)


def from_x(value, step):
    pairs = permutation(lambda y, z, x, c: (y, z, (x - step) % 4, c))
    return permute(value, pairs)


def from_core(value):
    return permute(value, permutation(lambda y, z, x, c: (y, z, x, 1 - c)))


def from_page(value, step):
    return permute(
        value,
        permutation(
            lambda y, z, x, c: (y, (z - step) % 4, x, c) if c == 0 else ((y - step) % 4, z, x, c)
        ),
    )


def from_query(value, step):
    return permute(
        value,
        permutation(
            lambda y, z, x, c: ((y - step) % 4, z, x, c) if c == 0 else (y, (z - step) % 4, x, c)
        ),
    )


def dot(a, b, a_dim, b_dim):
    return lax.dot_general(a, b, (((a_dim,), (b_dim,)), ((), ())), preferred_element_type=F32)


def tie(value, *others):
    return lax.optimization_barrier((value, others))[0]


def kernel_call(body, count, outs, scratch, flops, limit, away=(), tables=1):
    vmem, place = pl.BlockSpec(memory_space=pltpu.VMEM), pl.BlockSpec(memory_space=pltpu.HBM)
    return pl.pallas_call(
        body,
        grid_spec=pltpu.PrefetchScalarGridSpec(
            num_scalar_prefetch=tables,
            grid=(),
            in_specs=[place if n in away else vmem for n in range(count - tables)],
            out_specs=[vmem] * len(outs),
            scratch_shapes=scratch,
        ),
        out_shape=[jax.ShapeDtypeStruct(*out) for out in outs],
        compiler_params=pltpu.CompilerParams(vmem_limit_bytes=limit),
        cost_estimate=pl.CostEstimate(flops=flops, bytes_accessed=4 << 20, transcendentals=0),
    )


def project_kernel(base, pos, *refs):
    blocks = refs[:8]
    attn_gain, mlp_gain, w_hbm, cosine, sine, q_ref, kv_ref, mlp_ref = refs[8:16]
    weight, normed, centre_ref, inverse_ref, sem = refs[16:]
    rows = q_ref.shape[0]
    fetch = pltpu.make_async_copy(w_hbm, weight, sem)
    fetch.start()
    step = 16

    def at_rows(part):
        return pl.ds(pl.multiple_of(part * step, step), step)

    def twice(value):
        return jnp.concatenate([value, value], axis=1)

    def add_up(part, carry):
        at = at_rows(part)
        total = blocks[0][at, :].astype(F32)
        for block in blocks[1:]:
            total = total + block[at, :].astype(F32)
        centre_ref[at, :] = total[:, 0:128] + total[:, 128:256]
        return carry

    def square(part, carry):
        at = at_rows(part)
        centre = twice(centre_ref[at, :])
        total = None
        for block in blocks:
            value = block[at, :].astype(F32) - centre
            total = value * value if total is None else total + value * value
        inverse_ref[at, :] = total[:, 0:128] + total[:, 128:256]
        return carry

    def norm(part, carry):
        at = at_rows(part)
        centre, inverse = twice(centre_ref[at, :]), twice(inverse_ref[at, :])
        for n, block in enumerate(blocks):
            scaled = (block[at, :].astype(F32) - centre) * inverse
            normed[at, n * 256 : (n + 1) * 256] = (scaled * attn_gain[pos[n]]).astype(BF16)
            column = pl.multiple_of(pos[n] * 256, 256)
            mlp_ref[at, pl.ds(column, 256)] = (scaled * mlp_gain[pos[n]]).astype(BF16)
        return carry

    parts = rows // step
    lax.fori_loop(0, parts, add_up, 0, unroll=2)
    centre = jnp.sum(centre_ref[...], axis=-1, keepdims=True) * (1.0 / D)
    centre_ref[...] = jnp.broadcast_to(centre, centre_ref.shape)
    lax.fori_loop(0, parts, square, 0, unroll=2)
    inverse = lax.rsqrt(jnp.sum(inverse_ref[...], axis=-1, keepdims=True) * (1.0 / D) + 1e-05)
    inverse_ref[...] = jnp.broadcast_to(inverse, inverse_ref.shape)
    lax.fori_loop(0, parts, norm, 0, unroll=2)

    fetch.wait()

    def product(kind):
        mixed = None
        for n in range(8):
            row = pl.multiple_of(pos[n] * 256, 256)
            part = jnp.dot(
                normed[:, n * 256 : (n + 1) * 256],
                weight[pl.ds(row, 256), kind * 256 : (kind + 1) * 256],
                preferred_element_type=F32,
            )
            mixed = part if mixed is None else mixed + part
        return mixed

    lane = lax.broadcasted_iota(jnp.int32, (rows, 128), 1)

    def rotate(head):
        flipped = jnp.where(lane < ROT // 2, pltpu.roll(head, 96, 1), pltpu.roll(head, 32, 1))
        return head * cosine[base : base + rows, :] + flipped * sine[base : base + rows, :]

    scale = HD ** (-0.5)
    mixed = product(0)
    q_ref[:, 0:128] = (rotate(mixed[:, 0:128]) * scale).astype(BF16)
    q_ref[:, 128:256] = (mixed[:, 128:256] * scale).astype(BF16)
    mixed = product(1)
    kv_ref[:, 0:128] = rotate(mixed[:, 0:128]).astype(BF16)
    kv_ref[:, 128:256] = mixed[:, 128:256].astype(BF16)
    kv_ref[:, 256:512] = product(2).astype(BF16)


def project(base, pos, blocks, attn_gain, mlp_gain, weight, cosine, sine):
    rows = blocks[0].shape[0]
    return kernel_call(
        functools.partial(project_kernel, base),
        14,
        [((rows, 256), BF16), ((rows, 512), BF16), ((rows, D), BF16)],
        [
            pltpu.VMEM((D, 768), BF16),
            pltpu.VMEM((rows, D), BF16),
            pltpu.VMEM((rows, 128), F32),
            pltpu.VMEM((rows, 128), F32),
            pltpu.SemaphoreType.DMA,
        ],
        2 * rows * D * 768,
        LIMIT_PROJECT,
        away=(10,),
    )(pos, *blocks, attn_gain, mlp_gain, weight, cosine, sine)


def mlp_kernel(block, x_ref, up_ref, down_ref, out_ref, act):
    wide = 512

    def first(n, carry):
        at = pl.ds(pl.multiple_of(n * wide, wide), wide)
        value = jnp.dot(x_ref[...], up_ref[:, at], preferred_element_type=F32)
        value = value * (0.5 + 0.5 * lax.erf(value * (0.5**0.5)))
        act[:, at] = value.astype(BF16)
        return carry

    lax.fori_loop(0, FF_DEV // wide, first, 0)

    def second(n, carry):
        at = pl.ds(pl.multiple_of(block[n] * 256, 256), 256)
        out_ref[n] = jnp.dot(act[...], down_ref[:, at], preferred_element_type=F32).astype(BF16)
        return carry

    lax.fori_loop(0, 8, second, 0)


def mlp(block, x, up, down):
    rows = x.shape[0]
    return kernel_call(
        mlp_kernel,
        4,
        [((8, rows, 256), BF16)],
        [pltpu.VMEM((rows, FF_DEV), BF16)],
        8 * rows * D * 512,
        LIMIT_MLP,
    )(block, x, up, down)[0]


def request_value(starts, values, place):
    found = jnp.full(place.shape, values[0], jnp.int32)
    for j in range(1, 4):
        found = jnp.where(place >= starts[j], values[j], found)
    return found


def own_kernel(base, starts, q_ref, *refs):
    keys, (numer_ref, stat_ref) = refs[:-2], refs[-2:]
    rows = q_ref.shape[0]
    for t in range(rows // TILE):
        q = q_ref[t * TILE : (t + 1) * TILE, :]
        q_at = base + t * TILE
        place = q_at + lax.broadcasted_iota(jnp.int32, (1, TILE), 1)
        first = request_value(starts, [starts[j] for j in range(4)], place)
        spots = range(max(0, q_at - 2 * TILE), q_at + 1, TILE)
        scores = []
        for spot in spots:
            part = keys[spot // R][spot % R : spot % R + TILE, 0:256]
            score = dot(part, q, 1, 1)
            key_at = spot + lax.broadcasted_iota(jnp.int32, (TILE, TILE), 0)
            mine = q_at + lax.broadcasted_iota(jnp.int32, (TILE, TILE), 1)
            scores.append(jnp.where((key_at <= mine) & (key_at >= first), score, NEG))
        top = jnp.max(scores[0], axis=0, keepdims=True)
        for score in scores[1:]:
            top = jnp.maximum(top, jnp.max(score, axis=0, keepdims=True))
        total, numer = None, None
        for spot, score in zip(spots, scores):
            weight = jnp.exp(score - top)
            added = jnp.sum(weight, axis=0, keepdims=True)
            total = added if total is None else total + added
            part = keys[spot // R][spot % R : spot % R + TILE, 256:512]
            out = dot(part, weight.astype(BF16), 0, 0)
            numer = out if numer is None else numer + out
        numer_ref[:, t * TILE : (t + 1) * TILE] = numer
        stat_ref[0:1, t * TILE : (t + 1) * TILE] = top
        stat_ref[1:2, t * TILE : (t + 1) * TILE] = total


def own_attention(base, starts, q, keys):
    rows = q.shape[0]
    return kernel_call(
        functools.partial(own_kernel, base),
        len(keys) + 2,
        [((256, rows), F32), ((8, rows), F32)],
        [],
        4 * rows * 768 * 256,
        LIMIT_OWN,
    )(starts, q, *keys)


def prefix_kernel(base, seg, *refs):
    queries, pages, out = refs[0:4], refs[4:8], refs[8:12]
    q_buf, out_buf, items, counts, sem = refs[12:]
    copies = [pltpu.make_async_copy(queries[k], q_buf.at[k], sem.at[k]) for k in range(4)]
    for copy in copies:
        copy.start()
    for page in range(4):
        counts[page] = 0

    def sort(n, carry):
        page = seg[3 * n + 2]
        low = jnp.clip(seg[3 * n] - base, 0, R)
        high = jnp.clip(seg[3 * n + 1] - base, 0, R)

        @pl.when((page >= 0) & (high > low))
        def _():
            at = page * 16 + counts[page]
            items[at] = n
            counts[page] = counts[page] + 1

        return carry

    lax.fori_loop(0, 16, sort, 0)
    for copy in copies:
        copy.wait()

    for page in range(4):

        def request(spot, carry):
            n = items[page * 16 + spot]
            low = jnp.clip(seg[3 * n] - base, 0, R)
            high = jnp.clip(seg[3 * n + 1] - base, 0, R)
            k = n // 4

            def visit(t, inner):
                at = pl.multiple_of(t * TILE, TILE)
                here = pl.ds(at, TILE)
                score = dot(pages[page][:, 0:256], q_buf[k, here, :], 1, 1)
                top = jnp.max(score, axis=0, keepdims=True)
                weight = jnp.exp(score - top)
                total = jnp.sum(weight, axis=0, keepdims=True)
                numer = dot(pages[page][:, 256:512], weight.astype(BF16), 0, 0)
                part = numer * (1.0 / total)
                level = top + jnp.log(total)
                one = level.astype(BF16).astype(F32)
                two = (level - one).astype(BF16).astype(F32)
                three = level - one - two
                row = lax.broadcasted_iota(jnp.int32, (STAT, TILE), 0)
                stat = jnp.where(row == 0, one, jnp.where(row == 1, two, three))
                lane = at + lax.broadcasted_iota(jnp.int32, (1, TILE), 1)
                mine = (lane >= low) & (lane < high)
                old = out_buf[k, 0:256, here].astype(F32)
                out_buf[k, 0:256, here] = jnp.where(mine, part, old).astype(BF16)
                old = out_buf[k, 256 : 256 + STAT, here].astype(F32)
                out_buf[k, 256 : 256 + STAT, here] = jnp.where(mine, stat, old).astype(BF16)
                return inner

            lax.fori_loop(low // TILE, (high + TILE - 1) // TILE, visit, 0)
            return carry

        lax.fori_loop(0, counts[page], request, 0)
    backs = [pltpu.make_async_copy(out_buf.at[k], out[k], sem.at[k]) for k in range(4)]
    for copy in backs:
        copy.start()
    for copy in backs:
        copy.wait()


def prefix_attention(base, seg, queries, pages):
    return kernel_call(
        functools.partial(prefix_kernel, base),
        9,
        [((256 + STAT, R), BF16)] * 4,
        [
            pltpu.VMEM((4, R, 256), BF16),
            pltpu.VMEM((4, 256 + STAT, R), BF16),
            pltpu.SMEM((64,), jnp.int32),
            pltpu.SMEM((4,), jnp.int32),
            pltpu.SemaphoreType.DMA((4,)),
        ],
        4 * R * PREFIX * 512,
        LIMIT_PREFIX,
    )(seg, *queries, *pages)


def join_kernel(base, block, starts, numer_ref, stat_ref, b0, b1, b2, b3, w_ref, md_ref, att_ref, out_ref):
    place = base + lax.broadcasted_iota(jnp.int32, (1, R), 1)
    pick = request_value(starts, [starts[4 + j] for j in range(4)], place)
    part, level = None, None
    for k, back in enumerate((b0, b1, b2, b3)):
        here = back[0:256, :].astype(F32)
        mark = (
            back[256:257, :].astype(F32)
            + back[257:258, :].astype(F32)
            + back[258:259, :].astype(F32)
        )
        part = here if part is None else jnp.where(pick == k, here, part)
        level = mark if level is None else jnp.where(pick == k, mark, level)
    own_top = stat_ref[0:1, :]
    top = jnp.maximum(own_top, level)
    own = jnp.exp(own_top - top)
    far = jnp.exp(level - top)
    under = 1.0 / (stat_ref[1:2, :] * own + far)
    joined = numer_ref[...] * (own * under) + part * (far * under)
    att_ref[...] = jnp.transpose(joined).astype(BF16)

    def product(s, carry):
        at = pl.ds(pl.multiple_of(block[4 + s] * 256, 256), 256)
        value = jnp.dot(att_ref[...], w_ref[:, at], preferred_element_type=F32)
        out_ref[s] = (value + md_ref[4 + s].astype(F32)).astype(BF16)
        return carry

    lax.fori_loop(0, 4, product, 0)


def join(base, block, starts, numer, stat, backs, weight, md):
    return kernel_call(
        functools.partial(join_kernel, base),
        10,
        [((R, 256), BF16), ((4, R, 256), BF16)],
        [],
        2 * R * 1024 * 256,
        LIMIT_JOIN,
        tables=2,
    )(block, starts, numer, stat, *backs, weight, md)


def rest_kernel(block, att_ref, w_ref, md_ref, other_ref, *out):
    for s in range(4):
        at = pl.ds(pl.multiple_of(block[s] * 256, 256), 256)
        value = jnp.dot(att_ref[...], w_ref[:, at], preferred_element_type=F32)
        value = value + md_ref[s].astype(F32) + other_ref[s].astype(F32)
        out[s][...] = value.astype(BF16)


def rest(block, att, weight, md, other):
    return kernel_call(
        rest_kernel, 5, [((R, 256), BF16)] * 4, [], 2 * R * 1024 * 256, LIMIT_REST
    )(block, att, weight, md, other)


def shards(
    hidden_in,
    qkv_weight,
    dense_weight,
    up_weight,
    down_weight,
    attn_gain,
    mlp_gain,
    suffix_lengths,
    request_group,
    prefix_slot,
    prefix_cache,
):
    tok, head = lax.axis_index("tok"), lax.axis_index("head")
    y, z, x, c = tok // 4, tok % 4, head // 2, head % 2
    page_at, query_at = jnp.where(c == 0, z, y), jnp.where(c == 0, y, z)
    steps = jnp.arange(4, dtype=jnp.int32)

    pieces, near, before = [], [], hidden_in
    for n in range(NC):
        pieces.append(before[n * R : (n + 1) * R])
        near.append([pieces[n]] + [from_x(pieces[n], s) for s in (1, 2, 3)])
        before = tie(hidden_in, *near[-1])
    page = prefix_cache[0]
    pages = [page] + [from_page(page, s) for s in (1, 2, 3)]

    ends = jnp.cumsum(suffix_lengths, axis=1)
    starts = ends - suffix_lengths
    hit = request_group[:, :, None] == jnp.arange(16, dtype=jnp.int32)
    slots = jnp.sum(jnp.where(hit, prefix_slot, 0), axis=-1)
    my_starts = lax.dynamic_index_in_dim(starts, tok, 0, keepdims=False)
    my_slots = lax.dynamic_index_in_dim(slots, tok, 0, keepdims=False)
    my_picks = (jnp.where(c == 0, my_slots // 4, my_slots % 4) - query_at) % 4
    mine_of = jnp.concatenate([my_starts, my_picks]).astype(jnp.int32)
    places = jnp.arange(TOK, dtype=jnp.int32)
    first = request_value(my_starts, my_starts, places)
    position = (PREFIX + places - first).astype(F32)
    inverse = 10000.0 ** (-2.0 * jnp.arange(ROT // 2, dtype=F32) / ROT)
    lane = jnp.arange(128)
    spread = jnp.where(lane < ROT, jnp.tile(inverse, 4), 0.0)
    angle = position[:, None] * spread[None, :]
    cosine = jnp.cos(angle)
    sine = jnp.sin(angle) * jnp.where(lane < ROT // 2, -1.0, 1.0)

    line = (query_at + steps) % 4
    peers = jnp.where(c == 0, line * 4 + z, y * 4 + line)
    chosen = (peers[:, None] == jnp.arange(16, dtype=jnp.int32)).astype(jnp.int32)
    triple = jnp.stack([starts, ends, slots], axis=-1)
    triple = jnp.sum(chosen[:, :, None, None] * triple[None], axis=1)
    peer_slots = triple[:, :, 2]
    holder = jnp.where(c == 0, peer_slots // 4, peer_slots % 4)
    held = (jnp.where(c == 0, peer_slots % 4, peer_slots // 4) - page_at) % 4
    held = jnp.where(holder == query_at, held, -1)
    seg = jnp.concatenate([triple[:, :, 0:2], held[:, :, None]], axis=-1)
    seg = seg.reshape(-1).astype(jnp.int32)

    chips = (x + steps) % 4
    mine, theirs = chips * 2 + c, chips * 2 + 1 - c
    pos = jnp.concatenate([mine, theirs]).astype(jnp.int32)
    gains = [gain.reshape(8, 1, 256) for gain in (attn_gain, mlp_gain)]

    cosine, sine, seg, pos, mine_of = lax.optimization_barrier((cosine, sine, seg, pos, mine_of))
    q, kv, mlp_in = [None] * NC, [None] * NC, [None] * NC
    queries, md, own, backs = [None] * NC, [None] * NC, [None] * NC, [None] * NC
    for n in range(NC):
        group = near[n]
        ready = (cosine, seg) if n == 0 else (q[n - 1],)
        others = [from_core(group[0])] + [from_core(tie(group[s], *ready)) for s in (1, 2, 3)]
        blocks = group + others
        q[n], kv[n], mlp_in[n] = project(
            n * R, pos, blocks, *gains, qkv_weight, cosine, sine
        )
        queries[n] = [q[n]] + [from_query(q[n], s) for s in (1, 2, 3)]
    for n in range(NC):
        own[n] = own_attention(n * R, mine_of, q[n], kv[: n + 1])
    last = own[NC - 1][0]
    done, att, away = [], [None] * NC, [None] * NC
    for n in range(NC):
        queries[n][0] = tie(queries[n][0], last)
        parts = prefix_attention(n * R, seg, queries[n], pages)
        backs[n] = [parts[0]] + [from_query(parts[(4 - s) % 4], s) for s in (1, 2, 3)]
        last = parts[0]
    other, sums = [None] * NC, [None] * NC

    def finish(n):
        sums[n] = rest(pos, att[n], dense_weight, md[n], other[n])
        parts = [sums[n][0]] + [from_x(sums[n][s], (4 - s) % 4) for s in (1, 2, 3)]
        total = pieces[n].astype(F32)
        for part in parts:
            total = total + part.astype(F32)
        done.append(total.astype(BF16))

    for n in range(NC):
        md[n] = mlp(pos, tie(mlp_in[n], last), up_weight, down_weight)
        if n:
            finish(n - 1)
            last = sums[n - 1][0]
        numer, stat = own[n]
        att[n], away[n] = join(
            n * R, pos, mine_of, tie(numer, md[n], last), stat, backs[n], dense_weight, md[n]
        )
        other[n] = from_core(away[n])
        last = away[n]
    finish(NC - 1)
    kv[0] = tie(kv[0], *sums[NC - 1])
    return jnp.concatenate(done, axis=0), jnp.concatenate(kv, axis=0)


def solution(mesh):
    placed = (
        P("tok", "head"),
        P(None, "head"),
        P("head", None),
        P(None, "head"),
        P("head", None),
        P(),
        P(),
        P(),
        P(),
        P(),
        P("tok", None, "head"),
    )
    return jax.shard_map(
        shards,
        mesh=mesh,
        in_specs=placed,
        out_specs=(P("tok", "head"), P("tok", "head")),
        check_vma=False,
    )
```

profile of v0, /device:TPU:0, one launch (start us, length us, event | category | flops | bytes accessed | tf_op | source)
XLA Modules:
  0.0 152.3 jit_solution(10600712236313922812)
XLA Ops:
  1.7 2.9 %collective-permute-start = (bf16[512,256]{1,0:T(8,128)(2,1)S(1)}, bf16[512,256]{1,0:T(8,128)(2,1)S(1)}, u32[]{:S(2)}, u32[]{:S(2)}) collective-permute-start(bf16[512,256]{1,0:T(8,128)(2,1)S(1)} %slice.31.refs_0_), channel_id=1, source_target_pairs={{0,6},{1,7},{2,0},{3,1},{4,2},{5,3},{6,4},{7,5},{8,14},{9,15},{10,... | collective-permute-start | bytes 786440 | tf_op jit(solution)/shard_map/ppermute | solution.py:48
  10.2 2.5 %subtract_convert_fusion = f32[1024]{0:T(1024)S(1)} fusion(s32[]{:T(128)} %bitcast.3, s32[]{:T(128)} %bitcast.2, s32[]{:T(128)} %bitcast.1, s32[]{:T(128)} %bitcast), kind=kLoop, calls=%fused_computation.21 | loop fusion | flops 9216 | bytes 4112 | tf_op jit(solution)/shard_map/convert_element_type | solution.py:464
  12.7 1.9 %fusion = (f32[1024,128]{1,0:T(8,128)S(1)}, f32[1024,128]{1,0:T(8,128)S(1)}) fusion(f32[128]{0:T(128)S(1)} %get-tuple-element.112, f32[128]{0:T(128)S(1)} %get-tuple-element.113, f32[1024]{0:T(1024)S(1)} %subtract_convert_fusion), kind=kLoop, calls=%fused_computation.3 | loop fusion | flops 262144 | bytes 1053696 | tf_op jit(solution)/shard_map/mul | solution.py:470
  16.4 3.2 %collective-permute-done.2.refs_3_ = bf16[512,256]{1,0:T(8,128)(2,1)S(1)} collective-permute-done((bf16[512,256]{1,0:T(8,128)(2,1)S(1)}, bf16[512,256]{1,0:T(8,128)(2,1)S(1)}, u32[]{:S(2)}, u32[]{:S(2)}) %collective-permute-start.2) | collective-permute-done | bytes 262176 | tf_op jit(solution)/shard_map/ppermute | solution.py:48
  20.6 2.0 %collective-permute-start.8 = (bf16[512,256]{1,0:T(8,128)(2,1)S(1)}, bf16[512,256]{1,0:T(8,128)(2,1)S(1)}, u32[]{:S(2)}, u32[]{:S(2)}) collective-permute-start(bf16[512,256]{1,0:T(8,128)(2,1)S(1)} %slice.38.refs_0_), channel_id=1, source_target_pairs={{0,4},{1,5},{2,6},{3,7},{4,0},{5,1},{6,2},{7,3},{8,12},{9,13},{10,... | collective-permute-start | bytes 786440 | tf_op jit(solution)/shard_map/ppermute | solution.py:48
  22.7 1.4 collective-permute-start.7
  24.1 4.1 %collective-permute-start.17 = (bf16[1024,512]{1,0:T(8,128)(2,1)S(1)}, bf16[1024,512]{1,0:T(8,128)(2,1)S(1)}, u32[]{:S(2)}, u32[]{:S(2)}) collective-permute-start(bf16[1024,512]{1,0:T(8,128)(2,1)S(1)} %bitcast.10), channel_id=1, source_target_pairs={{0,24},{1,97},{2,26},{3,99},{4,28},{5,101},{6,30},{7,103},{8,0},{9... | collective-permute-start | bytes 3145736 | tf_op jit(solution)/shard_map/ppermute | solution.py:48
  28.2 8.0 %collective-permute-done.9.refs_3_ = bf16[512,256]{1,0:T(8,128)(2,1)S(1)} collective-permute-done((bf16[512,256]{1,0:T(8,128)(2,1)S(1)}, bf16[512,256]{1,0:T(8,128)(2,1)S(1)}, u32[]{:S(2)}, u32[]{:S(2)}) %collective-permute-start.9) | collective-permute-done | bytes 262176 | tf_op jit(solution)/shard_map/ppermute | solution.py:48
  36.1 3.9 %collective-permute-start.18 = (bf16[1024,512]{1,0:T(8,128)(2,1)S(1)}, bf16[1024,512]{1,0:T(8,128)(2,1)S(1)}, u32[]{:S(2)}, u32[]{:S(2)}) collective-permute-start(bf16[1024,512]{1,0:T(8,128)(2,1)S(1)} %bitcast.11), channel_id=1, source_target_pairs={{0,16},{1,65},{2,18},{3,67},{4,20},{5,69},{6,22},{7,71},{8,24},{9,... | collective-permute-start | bytes 3145736 | tf_op jit(solution)/shard_map/ppermute | solution.py:48
  41.0 1.9 %copy-done.1 = bf16[2048,768]{1,0:T(8,128)(2,1)S(1)} copy-done((bf16[2048,768]{1,0:T(8,128)(2,1)S(1)}, bf16[2048,768]{1,0:T(8,128)(2,1)}, u32[]{:S(2)}) %copy-start.1) | copy-done | bytes 3145752
  42.9 5.1 %shard_map.122 = (bf16[512,256]{1,0:T(8,128)(2,1)S(1)}, bf16[512,512]{1,0:T(8,128)(2,1)S(1)}, bf16[512,2048]{1,0:T(8,128)(2,1)S(1)}) custom-call(s32[8]{0:T(128)S(1)} %pad_add_fusion.2.pos.block, bf16[512,256]{1,0:T(8,128)(2,1)S(1)} %slice.31.refs_0_, bf16[512,256]{1,0:T(8,128)(2,1)S(1)} %collective-permute-done.refs_1_, ...), custom_call_target="tpu_custom_call" | custom-call | flops 1610612736 | bytes 4194304 | tf_op jit(solution)/shard_map/pallas_call | solution.py:187
  50.1 3.0 %collective-permute-start.14 = (bf16[512,256]{1,0:T(8,128)(2,1)S(1)}, bf16[512,256]{1,0:T(8,128)(2,1)S(1)}, u32[]{:S(2)}, u32[]{:S(2)}) collective-permute-start(bf16[512,256]{1,0:T(8,128)(2,1)S(1)} %get-tuple-element.70.q_ref.refs_0_), channel_id=1, source_target_pairs={{0,96},{1,25},{2,98},{3,27},{4,100},{5,29},{6,102},{7,31},{8,104},... | collective-permute-start | bytes 786440 | tf_op jit(solution)/shard_map/ppermute | solution.py:48
  54.4 5.4 %collective-permute-done.14.refs_1_ = bf16[512,256]{1,0:T(8,128)(2,1)S(1)} collective-permute-done((bf16[512,256]{1,0:T(8,128)(2,1)S(1)}, bf16[512,256]{1,0:T(8,128)(2,1)S(1)}, u32[]{:S(2)}, u32[]{:S(2)}) %collective-permute-start.14) | collective-permute-done | bytes 262176 | tf_op jit(solution)/shard_map/ppermute | solution.py:48
  59.8 5.1 %shard_map.124 = (bf16[512,256]{1,0:T(8,128)(2,1)S(1)}, bf16[512,512]{1,0:T(8,128)(2,1)S(1)}, bf16[512,2048]{1,0:T(8,128)(2,1)S(1)}) custom-call(s32[8]{0:T(128)S(1)} %pad_add_fusion.2.pos.block, bf16[512,256]{1,0:T(8,128)(2,1)S(1)} %slice.38.refs_0_, bf16[512,256]{1,0:T(8,128)(2,1)S(1)} %collective-permute-done.7.refs_1_, ...), custom_call_target="tpu_custom_call" | custom-call | flops 1610612736 | bytes 4194304 | tf_op jit(solution)/shard_map/pallas_call | solution.py:187
  64.9 3.8 %collective-permute-start.20 = (bf16[512,256]{1,0:T(8,128)(2,1)S(1)}, bf16[512,256]{1,0:T(8,128)(2,1)S(1)}, u32[]{:S(2)}, u32[]{:S(2)}) collective-permute-start(bf16[512,256]{1,0:T(8,128)(2,1)S(1)} %get-tuple-element.72.q_ref.refs_0_), channel_id=1, source_target_pairs={{0,96},{1,25},{2,98},{3,27},{4,100},{5,29},{6,102},{7,31},{8,104},... | collective-permute-start | bytes 786440 | tf_op jit(solution)/shard_map/ppermute | solution.py:48
  68.6 1.6 %collective-permute-start.21 = (bf16[512,256]{1,0:T(8,128)(2,1)S(1)}, bf16[512,256]{1,0:T(8,128)(2,1)S(1)}, u32[]{:S(2)}, u32[]{:S(2)}) collective-permute-start(bf16[512,256]{1,0:T(8,128)(2,1)S(1)} %get-tuple-element.72.q_ref.refs_0_), channel_id=1, source_target_pairs={{0,64},{1,17},{2,66},{3,19},{4,68},{5,21},{6,70},{7,23},{8,72},{9,... | collective-permute-start | bytes 786440 | tf_op jit(solution)/shard_map/ppermute | solution.py:48
  71.5 1.4 shard_map.123
  73.0 1.6 %shard_map.125 = (f32[256,512]{1,0:T(8,128)S(1)}, f32[8,512]{1,0:T(8,128)S(1)}) custom-call(s32[8]{0:T(128)S(1)} %pad_add_fusion.3.starts, bf16[512,256]{1,0:T(8,128)(2,1)S(1)} %get-tuple-element.72.q_ref.refs_0_, bf16[512,512]{1,0:T(8,128)(2,1)S(1)} %get-tuple-element.99.refs_0_, bf16[512,512]{1,0:T(8,128)(2,1)S(1)} %get-tuple-element.68.refs_1_), custom_call_target="tpu_custom_call" | custom-call | flops 402653184 | bytes 4194304 | tf_op jit(solution)/shard_map/pallas_call | solution.py:277
  74.6 10.2 %shard_map.126 = (bf16[272,512]{1,0:T(8,128)(2,1)S(1)}, bf16[272,512]{1,0:T(8,128)(2,1)S(1)}, bf16[272,512]{1,0:T(8,128)(2,1)S(1)}, bf16[272,512]{1,0:T(8,128)(2,1)S(1)}) custom-call(s32[48]{0:T(128)S(1)} %reshape.97.seg, bf16[512,256]{1,0:T(8,128)(2,1)S(1)} %get-tuple-element.70.q_ref.refs_0_, bf16[512,256]{1,0:T(8,128)(2,1)S(1)} %collective-permute-done.14.refs_1_, ...), custom_call_target="tpu_custom_call" | custom-call | flops 1073741824 | bytes 4194304 | tf_op jit(solution)/shard_map/pallas_call | solution.py:356
  84.9 11.2 %shard_map.127 = (bf16[272,512]{1,0:T(8,128)(2,1)S(1)}, bf16[272,512]{1,0:T(8,128)(2,1)S(1)}, bf16[272,512]{1,0:T(8,128)(2,1)S(1)}, bf16[272,512]{1,0:T(8,128)(2,1)S(1)}) custom-call(s32[48]{0:T(128)S(1)} %reshape.97.seg, bf16[512,256]{1,0:T(8,128)(2,1)S(1)} %get-tuple-element.72.q_ref.refs_0_, bf16[512,256]{1,0:T(8,128)(2,1)S(1)} %collective-permute-done.20.refs_1_, ...), custom_call_target="tpu_custom_call" | custom-call | flops 1073741824 | bytes 4194304 | tf_op jit(solution)/shard_map/pallas_call | solution.py:356
  96.3 1.9 %collective-permute-start.25 = (bf16[272,512]{1,0:T(8,128)(2,1)S(1)}, bf16[272,512]{1,0:T(8,128)(2,1)S(1)}, u32[]{:S(2)}, u32[]{:S(2)}) collective-permute-start(bf16[272,512]{1,0:T(8,128)(2,1)S(1)} %get-tuple-element.79), channel_id=1, source_target_pairs={{0,32},{1,9},{2,34},{3,11},{4,36},{5,13},{6,38},{7,15},{8,40},{9,1... | collective-permute-start | bytes 835592 | tf_op jit(solution)/shard_map/ppermute | solution.py:48
  98.3 6.8 %shard_map.128.md_ref = bf16[8,512,256]{2,1,0:T(8,128)(2,1)S(1)} custom-call(s32[8]{0:T(128)S(1)} %pad_add_fusion.2.pos.block, bf16[512,2048]{1,0:T(8,128)(2,1)S(1)} %get-tuple-element.74.x_ref, bf16[2048,1024]{1,0:T(8,128)(2,1)S(1)} %copy-done.6, bf16[1024,2048]{1,0:T(8,128)(2,1)S(1)} %copy-done.7), custom_call_target="tpu_custom_call" | custom-call | flops 4294967296 | bytes 4194304 | tf_op jit(solution)/shard_map/pallas_call | solution.py:226
  105.1 2.2 %collective-permute-done.25.b3 = bf16[272,512]{1,0:T(8,128)(2,1)S(1)} collective-permute-done((bf16[272,512]{1,0:T(8,128)(2,1)S(1)}, bf16[272,512]{1,0:T(8,128)(2,1)S(1)}, u32[]{:S(2)}, u32[]{:S(2)}) %collective-permute-start.25) | collective-permute-done | bytes 278560 | tf_op jit(solution)/shard_map/ppermute | solution.py:48
  107.4 1.8 %shard_map.129 = (bf16[512,256]{1,0:T(8,128)(2,1)S(1)}, bf16[4,512,256]{2,1,0:T(8,128)(2,1)S(1)}) custom-call(s32[8]{0:T(128)S(1)} %pad_add_fusion.2.pos.block, s32[8]{0:T(128)S(1)} %pad_add_fusion.3.starts, f32[256,512]{1,0:T(8,128)S(1)} %get-tuple-element.75.numer_ref, f32[8,512]{1,0:T(8,128)S(1)} %get-tuple-element.76.stat_ref, ...), custom_call_target="tpu_custom_call" | custom-call | flops 268435456 | bytes 4194304 | tf_op jit(solution)/shard_map/pallas_call | solution.py:403
  109.2 1.7 %collective-permute-start.30 = (bf16[272,512]{1,0:T(8,128)(2,1)S(1)}, bf16[272,512]{1,0:T(8,128)(2,1)S(1)}, u32[]{:S(2)}, u32[]{:S(2)}) collective-permute-start(bf16[272,512]{1,0:T(8,128)(2,1)S(1)} %get-tuple-element.90), channel_id=1, source_target_pairs={{0,96},{1,25},{2,98},{3,27},{4,100},{5,29},{6,102},{7,31},{8,104},... | collective-permute-start | bytes 835592 | tf_op jit(solution)/shard_map/ppermute | solution.py:48
  112.6 6.8 %shard_map.131.md_ref = bf16[8,512,256]{2,1,0:T(8,128)(2,1)S(1)} custom-call(s32[8]{0:T(128)S(1)} %pad_add_fusion.2.pos.block, bf16[512,2048]{1,0:T(8,128)(2,1)S(1)} %get-tuple-element.87.x_ref, bf16[2048,1024]{1,0:T(8,128)(2,1)S(1)} %copy-done.6, bf16[1024,2048]{1,0:T(8,128)(2,1)S(1)} %copy-done.7), custom_call_target="tpu_custom_call" | custom-call | flops 4294967296 | bytes 4194304 | tf_op jit(solution)/shard_map/pallas_call | solution.py:226
  120.6 1.4 collective-permute-done.32.b3
  122.0 1.8 %shard_map.132 = (bf16[512,256]{1,0:T(8,128)(2,1)S(1)}, bf16[4,512,256]{2,1,0:T(8,128)(2,1)S(1)}) custom-call(s32[8]{0:T(128)S(1)} %pad_add_fusion.2.pos.block, s32[8]{0:T(128)S(1)} %pad_add_fusion.3.starts, f32[256,512]{1,0:T(8,128)S(1)} %get-tuple-element.88.numer_ref, f32[8,512]{1,0:T(8,128)S(1)} %get-tuple-element.89.stat_ref, ...), custom_call_target="tpu_custom_call" | custom-call | flops 268435456 | bytes 4194304 | tf_op jit(solution)/shard_map/pallas_call | solution.py:403
  125.0 2.2 %collective-permute-start.29 = (bf16[512,256]{1,0:T(8,128)(2,1)S(1)}, bf16[512,256]{1,0:T(8,128)(2,1)S(1)}, u32[]{:S(2)}, u32[]{:S(2)}) collective-permute-start(bf16[512,256]{1,0:T(8,128)(2,1)S(1)} %get-tuple-element.85), channel_id=1, source_target_pairs={{0,6},{1,7},{2,0},{3,1},{4,2},{5,3},{6,4},{7,5},{8,14},{9,15},{10,... | collective-permute-start | bytes 786440 | tf_op jit(solution)/shard_map/ppermute | solution.py:48
  129.2 2.2 %collective-permute-start.35 = (bf16[512,256]{1,0:T(8,128)(2,1)S(1)}, bf16[512,256]{1,0:T(8,128)(2,1)S(1)}, u32[]{:S(2)}, u32[]{:S(2)}) collective-permute-start(bf16[512,256]{1,0:T(8,128)(2,1)S(1)} %get-tuple-element.97), channel_id=1, source_target_pairs={{0,4},{1,5},{2,6},{3,7},{4,0},{5,1},{6,2},{7,3},{8,12},{9,13},{10,... | collective-permute-start | bytes 786440 | tf_op jit(solution)/shard_map/ppermute | solution.py:48
  131.4 8.6 %collective-permute-done.27 = bf16[512,256]{1,0:T(8,128)(2,1)S(1)} collective-permute-done((bf16[512,256]{1,0:T(8,128)(2,1)S(1)}, bf16[512,256]{1,0:T(8,128)(2,1)S(1)}, u32[]{:S(2)}, u32[]{:S(2)}) %collective-permute-start.27) | collective-permute-done | bytes 262176 | tf_op jit(solution)/shard_map/ppermute | solution.py:48
  142.1 8.6 %collective-permute-done.34 = bf16[512,256]{1,0:T(8,128)(2,1)S(1)} collective-permute-done((bf16[512,256]{1,0:T(8,128)(2,1)S(1)}, bf16[512,256]{1,0:T(8,128)(2,1)S(1)}, u32[]{:S(2)}, u32[]{:S(2)}) %collective-permute-start.34) | collective-permute-done | bytes 262176 | tf_op jit(solution)/shard_map/ppermute | solution.py:48
  (102 shorter events, 25.1 us)
Async XLA Ops:
  1.7 14.1 %collective-permute-start = (bf16[512,256]{1,0:T(8,128)(2,1)S(1)}, bf16[512,256]{1,0:T(8,128)(2,1)S(1)}, u32[]{:S(2)}, u32[]{:S(2)}) collective-permute-start(bf16[512,256]{1,0:T(8,128)(2,1)S(1)} %slice.31.refs_0_), channel_id=1, source_target_pairs={{0,6},{1,7},{2,0},{3,1},{4,2},{5,3},{6,4},{7,5},{8,14},{9,15},{10,... | collective-permute-start | bytes 786440 | tf_op jit(solution)/shard_map/ppermute | solution.py:48
  4.7 11.2 %collective-permute-start.1 = (bf16[512,256]{1,0:T(8,128)(2,1)S(1)}, bf16[512,256]{1,0:T(8,128)(2,1)S(1)}, u32[]{:S(2)}, u32[]{:S(2)}) collective-permute-start(bf16[512,256]{1,0:T(8,128)(2,1)S(1)} %slice.31.refs_0_), channel_id=1, source_target_pairs={{0,4},{1,5},{2,6},{3,7},{4,0},{5,1},{6,2},{7,3},{8,12},{9,13},{10,... | collective-permute-start | bytes 786440 | tf_op jit(solution)/shard_map/ppermute | solution.py:48
  5.5 14.1 %collective-permute-start.2 = (bf16[512,256]{1,0:T(8,128)(2,1)S(1)}, bf16[512,256]{1,0:T(8,128)(2,1)S(1)}, u32[]{:S(2)}, u32[]{:S(2)}) collective-permute-start(bf16[512,256]{1,0:T(8,128)(2,1)S(1)} %slice.31.refs_0_), channel_id=1, source_target_pairs={{0,2},{1,3},{2,4},{3,5},{4,6},{5,7},{6,0},{7,1},{8,10},{9,11},{10,... | collective-permute-start | bytes 786440 | tf_op jit(solution)/shard_map/ppermute | solution.py:48
  6.3 14.3 %collective-permute-start.3 = (bf16[512,256]{1,0:T(8,128)(2,1)S(1)}, bf16[512,256]{1,0:T(8,128)(2,1)S(1)}, u32[]{:S(2)}, u32[]{:S(2)}) collective-permute-start(bf16[512,256]{1,0:T(8,128)(2,1)S(1)} %slice.31.refs_0_), channel_id=1, source_target_pairs={{0,1},{1,0},{2,3},{3,2},{4,5},{5,4},{6,7},{7,6},{8,9},{9,8},{10,11... | collective-permute-start | bytes 786440 | tf_op jit(solution)/shard_map/ppermute | solution.py:48
  15.8 6.8 %collective-permute-start.4 = (bf16[512,256]{1,0:T(8,128)(2,1)S(1)}, bf16[512,256]{1,0:T(8,128)(2,1)S(1)}, u32[]{:S(2)}, u32[]{:S(2)}) collective-permute-start(bf16[512,256]{1,0:T(8,128)(2,1)S(1)} %collective-permute-done.refs_1_), channel_id=1, source_target_pairs={{0,1},{1,0},{2,3},{3,2},{4,5},{5,4},{6,7},{7,6},{8,9},{9,8},{10,11... | collective-permute-start | bytes 786440 | tf_op jit(solution)/shard_map/ppermute | solution.py:48
  15.8 8.2 %collective-permute-start.5 = (bf16[512,256]{1,0:T(8,128)(2,1)S(1)}, bf16[512,256]{1,0:T(8,128)(2,1)S(1)}, u32[]{:S(2)}, u32[]{:S(2)}) collective-permute-start(bf16[512,256]{1,0:T(8,128)(2,1)S(1)} %collective-permute-done.1.refs_2_), channel_id=1, source_target_pairs={{0,1},{1,0},{2,3},{3,2},{4,5},{5,4},{6,7},{7,6},{8,9},{9,8},{10,11... | collective-permute-start | bytes 786440 | tf_op jit(solution)/shard_map/ppermute | solution.py:48
  20.5 15.6 %collective-permute-start.9 = (bf16[512,256]{1,0:T(8,128)(2,1)S(1)}, bf16[512,256]{1,0:T(8,128)(2,1)S(1)}, u32[]{:S(2)}, u32[]{:S(2)}) collective-permute-start(bf16[512,256]{1,0:T(8,128)(2,1)S(1)} %slice.38.refs_0_), channel_id=1, source_target_pairs={{0,2},{1,3},{2,4},{3,5},{4,6},{5,7},{6,0},{7,1},{8,10},{9,11},{10,... | collective-permute-start | bytes 786440 | tf_op jit(solution)/shard_map/ppermute | solution.py:48
  20.6 19.4 %collective-permute-start.8 = (bf16[512,256]{1,0:T(8,128)(2,1)S(1)}, bf16[512,256]{1,0:T(8,128)(2,1)S(1)}, u32[]{:S(2)}, u32[]{:S(2)}) collective-permute-start(bf16[512,256]{1,0:T(8,128)(2,1)S(1)} %slice.38.refs_0_), channel_id=1, source_target_pairs={{0,4},{1,5},{2,6},{3,7},{4,0},{5,1},{6,2},{7,3},{8,12},{9,13},{10,... | collective-permute-start | bytes 786440 | tf_op jit(solution)/shard_map/ppermute | solution.py:48
  22.7 25.4 %collective-permute-start.7 = (bf16[512,256]{1,0:T(8,128)(2,1)S(1)}, bf16[512,256]{1,0:T(8,128)(2,1)S(1)}, u32[]{:S(2)}, u32[]{:S(2)}) collective-permute-start(bf16[512,256]{1,0:T(8,128)(2,1)S(1)} %slice.38.refs_0_), channel_id=1, source_target_pairs={{0,6},{1,7},{2,0},{3,1},{4,2},{5,3},{6,4},{7,5},{8,14},{9,15},{10,... | collective-permute-start | bytes 786440 | tf_op jit(solution)/shard_map/ppermute | solution.py:48
  24.0 24.1 %collective-permute-start.10 = (bf16[512,256]{1,0:T(8,128)(2,1)S(1)}, bf16[512,256]{1,0:T(8,128)(2,1)S(1)}, u32[]{:S(2)}, u32[]{:S(2)}) collective-permute-start(bf16[512,256]{1,0:T(8,128)(2,1)S(1)} %slice.38.refs_0_), channel_id=1, source_target_pairs={{0,1},{1,0},{2,3},{3,2},{4,5},{5,4},{6,7},{7,6},{8,9},{9,8},{10,11... | collective-permute-start | bytes 786440 | tf_op jit(solution)/shard_map/ppermute | solution.py:48
  24.1 46.1 %collective-permute-start.17 = (bf16[1024,512]{1,0:T(8,128)(2,1)S(1)}, bf16[1024,512]{1,0:T(8,128)(2,1)S(1)}, u32[]{:S(2)}, u32[]{:S(2)}) collective-permute-start(bf16[1024,512]{1,0:T(8,128)(2,1)S(1)} %bitcast.10), channel_id=1, source_target_pairs={{0,24},{1,97},{2,26},{3,99},{4,28},{5,101},{6,30},{7,103},{8,0},{9... | collective-permute-start | bytes 3145736 | tf_op jit(solution)/shard_map/ppermute | solution.py:48
  36.1 38.5 %collective-permute-start.18 = (bf16[1024,512]{1,0:T(8,128)(2,1)S(1)}, bf16[1024,512]{1,0:T(8,128)(2,1)S(1)}, u32[]{:S(2)}, u32[]{:S(2)}) collective-permute-start(bf16[1024,512]{1,0:T(8,128)(2,1)S(1)} %bitcast.11), channel_id=1, source_target_pairs={{0,16},{1,65},{2,18},{3,67},{4,20},{5,69},{6,22},{7,71},{8,24},{9,... | collective-permute-start | bytes 3145736 | tf_op jit(solution)/shard_map/ppermute | solution.py:48
  40.0 34.6 %collective-permute-start.19 = (bf16[1024,512]{1,0:T(8,128)(2,1)S(1)}, bf16[1024,512]{1,0:T(8,128)(2,1)S(1)}, u32[]{:S(2)}, u32[]{:S(2)}) collective-permute-start(bf16[1024,512]{1,0:T(8,128)(2,1)S(1)} %bitcast.12), channel_id=1, source_target_pairs={{0,8},{1,33},{2,10},{3,35},{4,12},{5,37},{6,14},{7,39},{8,16},{9,4... | collective-permute-start | bytes 3145736 | tf_op jit(solution)/shard_map/ppermute | solution.py:48
  50.1 9.7 %collective-permute-start.14 = (bf16[512,256]{1,0:T(8,128)(2,1)S(1)}, bf16[512,256]{1,0:T(8,128)(2,1)S(1)}, u32[]{:S(2)}, u32[]{:S(2)}) collective-permute-start(bf16[512,256]{1,0:T(8,128)(2,1)S(1)} %get-tuple-element.70.q_ref.refs_0_), channel_id=1, source_target_pairs={{0,96},{1,25},{2,98},{3,27},{4,100},{5,29},{6,102},{7,31},{8,104},... | collective-permute-start | bytes 786440 | tf_op jit(solution)/shard_map/ppermute | solution.py:48
  53.1 11.8 %collective-permute-start.15 = (bf16[512,256]{1,0:T(8,128)(2,1)S(1)}, bf16[512,256]{1,0:T(8,128)(2,1)S(1)}, u32[]{:S(2)}, u32[]{:S(2)}) collective-permute-start(bf16[512,256]{1,0:T(8,128)(2,1)S(1)} %get-tuple-element.70.q_ref.refs_0_), channel_id=1, source_target_pairs={{0,64},{1,17},{2,66},{3,19},{4,68},{5,21},{6,70},{7,23},{8,72},{9,... | collective-permute-start | bytes 786440 | tf_op jit(solution)/shard_map/ppermute | solution.py:48
  59.8 8.9 %collective-permute-start.16 = (bf16[512,256]{1,0:T(8,128)(2,1)S(1)}, bf16[512,256]{1,0:T(8,128)(2,1)S(1)}, u32[]{:S(2)}, u32[]{:S(2)}) collective-permute-start(bf16[512,256]{1,0:T(8,128)(2,1)S(1)} %get-tuple-element.70.q_ref.refs_0_), channel_id=1, source_target_pairs={{0,32},{1,9},{2,34},{3,11},{4,36},{5,13},{6,38},{7,15},{8,40},{9,1... | collective-permute-start | bytes 786440 | tf_op jit(solution)/shard_map/ppermute | solution.py:48
  64.9 20.0 %collective-permute-start.20 = (bf16[512,256]{1,0:T(8,128)(2,1)S(1)}, bf16[512,256]{1,0:T(8,128)(2,1)S(1)}, u32[]{:S(2)}, u32[]{:S(2)}) collective-permute-start(bf16[512,256]{1,0:T(8,128)(2,1)S(1)} %get-tuple-element.72.q_ref.refs_0_), channel_id=1, source_target_pairs={{0,96},{1,25},{2,98},{3,27},{4,100},{5,29},{6,102},{7,31},{8,104},... | collective-permute-start | bytes 786440 | tf_op jit(solution)/shard_map/ppermute | solution.py:48
  68.6 16.2 %collective-permute-start.21 = (bf16[512,256]{1,0:T(8,128)(2,1)S(1)}, bf16[512,256]{1,0:T(8,128)(2,1)S(1)}, u32[]{:S(2)}, u32[]{:S(2)}) collective-permute-start(bf16[512,256]{1,0:T(8,128)(2,1)S(1)} %get-tuple-element.72.q_ref.refs_0_), channel_id=1, source_target_pairs={{0,64},{1,17},{2,66},{3,19},{4,68},{5,21},{6,70},{7,23},{8,72},{9,... | collective-permute-start | bytes 786440 | tf_op jit(solution)/shard_map/ppermute | solution.py:48
  70.2 14.7 %collective-permute-start.22 = (bf16[512,256]{1,0:T(8,128)(2,1)S(1)}, bf16[512,256]{1,0:T(8,128)(2,1)S(1)}, u32[]{:S(2)}, u32[]{:S(2)}) collective-permute-start(bf16[512,256]{1,0:T(8,128)(2,1)S(1)} %get-tuple-element.72.q_ref.refs_0_), channel_id=1, source_target_pairs={{0,32},{1,9},{2,34},{3,11},{4,36},{5,13},{6,38},{7,15},{8,40},{9,1... | collective-permute-start | bytes 786440 | tf_op jit(solution)/shard_map/ppermute | solution.py:48
  96.2 8.9 %collective-permute-start.23 = (bf16[272,512]{1,0:T(8,128)(2,1)S(1)}, bf16[272,512]{1,0:T(8,128)(2,1)S(1)}, u32[]{:S(2)}, u32[]{:S(2)}) collective-permute-start(bf16[272,512]{1,0:T(8,128)(2,1)S(1)} %get-tuple-element.77), channel_id=1, source_target_pairs={{0,96},{1,25},{2,98},{3,27},{4,100},{5,29},{6,102},{7,31},{8,104},... | collective-permute-start | bytes 835592 | tf_op jit(solution)/shard_map/ppermute | solution.py:48
  96.2 8.9 %collective-permute-start.24 = (bf16[272,512]{1,0:T(8,128)(2,1)S(1)}, bf16[272,512]{1,0:T(8,128)(2,1)S(1)}, u32[]{:S(2)}, u32[]{:S(2)}) collective-permute-start(bf16[272,512]{1,0:T(8,128)(2,1)S(1)} %get-tuple-element.78), channel_id=1, source_target_pairs={{0,64},{1,17},{2,66},{3,19},{4,68},{5,21},{6,70},{7,23},{8,72},{9,... | collective-permute-start | bytes 835592 | tf_op jit(solution)/shard_map/ppermute | solution.py:48
  96.3 11.0 %collective-permute-start.25 = (bf16[272,512]{1,0:T(8,128)(2,1)S(1)}, bf16[272,512]{1,0:T(8,128)(2,1)S(1)}, u32[]{:S(2)}, u32[]{:S(2)}) collective-permute-start(bf16[272,512]{1,0:T(8,128)(2,1)S(1)} %get-tuple-element.79), channel_id=1, source_target_pairs={{0,32},{1,9},{2,34},{3,11},{4,36},{5,13},{6,38},{7,15},{8,40},{9,1... | collective-permute-start | bytes 835592 | tf_op jit(solution)/shard_map/ppermute | solution.py:48
  109.1 10.3 %collective-permute-start.26 = (bf16[4,512,256]{2,1,0:T(8,128)(2,1)S(1)}, bf16[4,512,256]{2,1,0:T(8,128)(2,1)S(1)}, u32[]{:S(2)}, u32[]{:S(2)}) collective-permute-start(bf16[4,512,256]{2,1,0:T(8,128)(2,1)S(1)} %get-tuple-element.81), channel_id=1, source_target_pairs={{0,1},{1,0},{2,3},{3,2},{4,5},{5,4},{6,7},{7,6},{8,9},{9,8},{10,11... | collective-permute-start | bytes 3145736 | tf_op jit(solution)/shard_map/ppermute | solution.py:48
  109.2 11.4 %collective-permute-start.30 = (bf16[272,512]{1,0:T(8,128)(2,1)S(1)}, bf16[272,512]{1,0:T(8,128)(2,1)S(1)}, u32[]{:S(2)}, u32[]{:S(2)}) collective-permute-start(bf16[272,512]{1,0:T(8,128)(2,1)S(1)} %get-tuple-element.90), channel_id=1, source_target_pairs={{0,96},{1,25},{2,98},{3,27},{4,100},{5,29},{6,102},{7,31},{8,104},... | collective-permute-start | bytes 835592 | tf_op jit(solution)/shard_map/ppermute | solution.py:48
  110.9 9.6 %collective-permute-start.31 = (bf16[272,512]{1,0:T(8,128)(2,1)S(1)}, bf16[272,512]{1,0:T(8,128)(2,1)S(1)}, u32[]{:S(2)}, u32[]{:S(2)}) collective-permute-start(bf16[272,512]{1,0:T(8,128)(2,1)S(1)} %get-tuple-element.91), channel_id=1, source_target_pairs={{0,64},{1,17},{2,66},{3,19},{4,68},{5,21},{6,70},{7,23},{8,72},{9,... | collective-permute-start | bytes 835592 | tf_op jit(solution)/shard_map/ppermute | solution.py:48
  111.3 10.7 %collective-permute-start.32 = (bf16[272,512]{1,0:T(8,128)(2,1)S(1)}, bf16[272,512]{1,0:T(8,128)(2,1)S(1)}, u32[]{:S(2)}, u32[]{:S(2)}) collective-permute-start(bf16[272,512]{1,0:T(8,128)(2,1)S(1)} %get-tuple-element.92), channel_id=1, source_target_pairs={{0,32},{1,9},{2,34},{3,11},{4,36},{5,13},{6,38},{7,15},{8,40},{9,1... | collective-permute-start | bytes 835592 | tf_op jit(solution)/shard_map/ppermute | solution.py:48
  123.9 16.1 %collective-permute-start.27 = (bf16[512,256]{1,0:T(8,128)(2,1)S(1)}, bf16[512,256]{1,0:T(8,128)(2,1)S(1)}, u32[]{:S(2)}, u32[]{:S(2)}) collective-permute-start(bf16[512,256]{1,0:T(8,128)(2,1)S(1)} %get-tuple-element.83), channel_id=1, source_target_pairs={{0,2},{1,3},{2,4},{3,5},{4,6},{5,7},{6,0},{7,1},{8,10},{9,11},{10,... | collective-permute-start | bytes 786440 | tf_op jit(solution)/shard_map/ppermute | solution.py:48
  123.9 16.0 %collective-permute-start.28 = (bf16[512,256]{1,0:T(8,128)(2,1)S(1)}, bf16[512,256]{1,0:T(8,128)(2,1)S(1)}, u32[]{:S(2)}, u32[]{:S(2)}) collective-permute-start(bf16[512,256]{1,0:T(8,128)(2,1)S(1)} %get-tuple-element.84), channel_id=1, source_target_pairs={{0,4},{1,5},{2,6},{3,7},{4,0},{5,1},{6,2},{7,3},{8,12},{9,13},{10,... | collective-permute-start | bytes 786440 | tf_op jit(solution)/shard_map/ppermute | solution.py:48
  125.0 15.9 %collective-permute-start.29 = (bf16[512,256]{1,0:T(8,128)(2,1)S(1)}, bf16[512,256]{1,0:T(8,128)(2,1)S(1)}, u32[]{:S(2)}, u32[]{:S(2)}) collective-permute-start(bf16[512,256]{1,0:T(8,128)(2,1)S(1)} %get-tuple-element.85), channel_id=1, source_target_pairs={{0,6},{1,7},{2,0},{3,1},{4,2},{5,3},{6,4},{7,5},{8,14},{9,15},{10,... | collective-permute-start | bytes 786440 | tf_op jit(solution)/shard_map/ppermute | solution.py:48
  128.3 22.3 %collective-permute-start.34 = (bf16[512,256]{1,0:T(8,128)(2,1)S(1)}, bf16[512,256]{1,0:T(8,128)(2,1)S(1)}, u32[]{:S(2)}, u32[]{:S(2)}) collective-permute-start(bf16[512,256]{1,0:T(8,128)(2,1)S(1)} %get-tuple-element.96), channel_id=1, source_target_pairs={{0,2},{1,3},{2,4},{3,5},{4,6},{5,7},{6,0},{7,1},{8,10},{9,11},{10,... | collective-permute-start | bytes 786440 | tf_op jit(solution)/shard_map/ppermute | solution.py:48
  129.2 21.4 %collective-permute-start.35 = (bf16[512,256]{1,0:T(8,128)(2,1)S(1)}, bf16[512,256]{1,0:T(8,128)(2,1)S(1)}, u32[]{:S(2)}, u32[]{:S(2)}) collective-permute-start(bf16[512,256]{1,0:T(8,128)(2,1)S(1)} %get-tuple-element.97), channel_id=1, source_target_pairs={{0,4},{1,5},{2,6},{3,7},{4,0},{5,1},{6,2},{7,3},{8,12},{9,13},{10,... | collective-permute-start | bytes 786440 | tf_op jit(solution)/shard_map/ppermute | solution.py:48
  139.9 11.4 %collective-permute-start.36 = (bf16[512,256]{1,0:T(8,128)(2,1)S(1)}, bf16[512,256]{1,0:T(8,128)(2,1)S(1)}, u32[]{:S(2)}, u32[]{:S(2)}) collective-permute-start(bf16[512,256]{1,0:T(8,128)(2,1)S(1)} %get-tuple-element.98), channel_id=1, source_target_pairs={{0,6},{1,7},{2,0},{3,1},{4,2},{5,3},{6,4},{7,5},{8,14},{9,15},{10,... | collective-permute-start | bytes 786440 | tf_op jit(solution)/shard_map/ppermute | solution.py:48
  (14 other events, 199.5 us)
where the time goes:
time: 153 us; the launch traced here: 152 us
  Pallas kernels  54.1 us (35%)
  starting transfers between devices  41.4 us (27%)
  waiting for transfers between devices  41 us (27%)
  other arithmetic  9.53 us (6%)
  local copies, waits for them, and re-layouts  5.2 us (3%)
    ppermute x37, starting transfers between devices, permute(): return lax.ppermute(value, BOTH, pairs)  41.4 us
    ppermute x37, waiting for transfers between devices, permute(): return lax.ppermute(value, BOTH, pairs)  41 us
    pallas_call x2, Pallas kernels, prefix_attention(): kernel_call(functools.partial(prefix_kernel, base), 9, [((256 + STAT, R),...  21.5 us
    pallas_call x2, Pallas kernels, mlp(): kernel_call(mlp_kernel, 4, [((8, rows, 256), BF16)], [pltpu.VMEM((rows, F...  13.6 us
    pallas_call x2, Pallas kernels, project(): kernel_call(functools.partial(project_kernel, base), 14, [((rows, 256), B...  10.2 us
    pallas_call x2, Pallas kernels, join(): kernel_call(functools.partial(join_kernel, base), 10, [((R, 256), BF16),...  3.54 us
    pallas_call x2, Pallas kernels, own_attention(): kernel_call(functools.partial(own_kernel, base), len(keys) + 2, [((256, r...  3.06 us
  transfers between devices with their start and end apart: 37, of which 12 were waited for; matrix products, arithmetic and copies ran while one was open for 7% of the time, Pallas kernels for 26%

commit v1 on v0

--- a/solution.py
+++ b/solution.py
@@ -2,6 +2,7 @@
 
 import jax
 import jax.numpy as jnp
+import numpy as np
 from jax import lax
 from jax.experimental import pallas as pl
 from jax.experimental.pallas import tpu as pltpu
@@ -22,12 +23,12 @@
 BF16 = jnp.bfloat16
 NEG = -1e30
 MIB = 1 << 20
-LIMIT_MLP = 18 * MIB
-LIMIT_PROJECT = 16 * MIB
-LIMIT_OWN = 10 * MIB
-LIMIT_PREFIX = 16 * MIB
-LIMIT_JOIN = 12 * MIB
-LIMIT_REST = 10 * MIB
+LIMIT_MLP = 12 * MIB
+LIMIT_PROJECT = 12 * MIB
+LIMIT_OWN = 6 * MIB
+LIMIT_PREFIX = 12 * MIB
+LIMIT_JOIN = 6 * MIB
+LIMIT_REST = 6 * MIB
 
 
 def flat(y, z, x, c):
@@ -102,11 +103,9 @@
 
 def project_kernel(base, pos, *refs):
     blocks = refs[:8]
-    attn_gain, mlp_gain, w_hbm, cosine, sine, q_ref, kv_ref, mlp_ref = refs[8:16]
-    weight, normed, centre_ref, inverse_ref, sem = refs[16:]
+    attn_gain, mlp_gain, weight, cosine, sine, q_ref, kv_ref, mlp_ref = refs[8:16]
+    normed, centre_ref, inverse_ref = refs[16:]
     rows = q_ref.shape[0]
-    fetch = pltpu.make_async_copy(w_hbm, weight, sem)
-    fetch.start()
     step = 16
 
     def at_rows(part):
@@ -151,8 +150,6 @@
     inverse = lax.rsqrt(jnp.sum(inverse_ref[...], axis=-1, keepdims=True) * (1.0 / D) + 1e-05)
     inverse_ref[...] = jnp.broadcast_to(inverse, inverse_ref.shape)
     lax.fori_loop(0, parts, norm, 0, unroll=2)
-
-    fetch.wait()
 
     def product(kind):
         mixed = None
@@ -189,15 +186,12 @@
         14,
         [((rows, 256), BF16), ((rows, 512), BF16), ((rows, D), BF16)],
         [
-            pltpu.VMEM((D, 768), BF16),
             pltpu.VMEM((rows, D), BF16),
             pltpu.VMEM((rows, 128), F32),
             pltpu.VMEM((rows, 128), F32),
-            pltpu.SemaphoreType.DMA,
         ],
         2 * rows * D * 768,
         LIMIT_PROJECT,
-        away=(10,),
     )(pos, *blocks, attn_gain, mlp_gain, weight, cosine, sine)
 
 
@@ -318,14 +312,25 @@
             high = jnp.clip(seg[3 * n + 1] - base, 0, R)
             k = n // 4
 
+            begin = jnp.minimum(low // 128 * 128, R - TILE)
+
             def visit(t, inner):
-                at = pl.multiple_of(t * TILE, TILE)
+                at = pl.multiple_of(jnp.minimum(begin + t * TILE, R - TILE), 128)
                 here = pl.ds(at, TILE)
-                score = dot(pages[page][:, 0:256], q_buf[k, here, :], 1, 1)
-                top = jnp.max(score, axis=0, keepdims=True)
-                weight = jnp.exp(score - top)
-                total = jnp.sum(weight, axis=0, keepdims=True)
-                numer = dot(pages[page][:, 256:512], weight.astype(BF16), 0, 0)
+                q = q_buf[k, here, :]
+                half = PREFIX // 2
+                scores = [dot(pages[page][h * half : (h + 1) * half, 0:256], q, 1, 1) for h in range(2)]
+                tops = [jnp.max(score, axis=0, keepdims=True) for score in scores]
+                weights = [jnp.exp(score - top) for score, top in zip(scores, tops)]
+                totals = [jnp.sum(weight, axis=0, keepdims=True) for weight in weights]
+                numers = [
+                    dot(pages[page][h * half : (h + 1) * half, 256:512], weight.astype(BF16), 0, 0)
+                    for h, weight in enumerate(weights)
+                ]
+                top = jnp.maximum(tops[0], tops[1])
+                shares = [jnp.exp(value - top) for value in tops]
+                total = totals[0] * shares[0] + totals[1] * shares[1]
+                numer = numers[0] * shares[0] + numers[1] * shares[1]
                 part = numer * (1.0 / total)
                 level = top + jnp.log(total)
                 one = level.astype(BF16).astype(F32)
@@ -341,7 +346,7 @@
                 out_buf[k, 256 : 256 + STAT, here] = jnp.where(mine, stat, old).astype(BF16)
                 return inner
 
-            lax.fori_loop(low // TILE, (high + TILE - 1) // TILE, visit, 0)
+            lax.fori_loop(0, (high - begin + TILE - 1) // TILE, visit, 0)
             return carry
 
         lax.fori_loop(0, counts[page], request, 0)
@@ -451,7 +456,8 @@
     page = prefix_cache[0]
     pages = [page] + [from_page(page, s) for s in (1, 2, 3)]
 
-    ends = jnp.cumsum(suffix_lengths, axis=1)
+    upto = (steps[None, :] <= steps[:, None]).astype(jnp.int32)
+    ends = jnp.sum(suffix_lengths[:, None, :] * upto[None], axis=-1)
     starts = ends - suffix_lengths
     hit = request_group[:, :, None] == jnp.arange(16, dtype=jnp.int32)
     slots = jnp.sum(jnp.where(hit, prefix_slot, 0), axis=-1)
@@ -460,12 +466,13 @@
     my_picks = (jnp.where(c == 0, my_slots // 4, my_slots % 4) - query_at) % 4
     mine_of = jnp.concatenate([my_starts, my_picks]).astype(jnp.int32)
     places = jnp.arange(TOK, dtype=jnp.int32)
-    first = request_value(my_starts, my_starts, places)
+    later = jnp.where(places[None, :] >= my_starts[:, None], my_starts[:, None], 0)
+    first = jnp.max(later, axis=0)
     position = (PREFIX + places - first).astype(F32)
-    inverse = 10000.0 ** (-2.0 * jnp.arange(ROT // 2, dtype=F32) / ROT)
     lane = jnp.arange(128)
-    spread = jnp.where(lane < ROT, jnp.tile(inverse, 4), 0.0)
-    angle = position[:, None] * spread[None, :]
+    rates = np.zeros((1, 128), np.float32)
+    rates[0, :ROT] = np.tile(10000.0 ** (-2.0 * np.arange(ROT // 2) / ROT), 2)
+    angle = position[:, None] * rates
     cosine = jnp.cos(angle)
     sine = jnp.sin(angle) * jnp.where(lane < ROT // 2, -1.0, 1.0)
 

time: 153 us -> 149 us (0.974)
  Pallas kernels: 54.1 us -> 50.7 us
  waiting for transfers between devices: 41 us -> 43.2 us
  other arithmetic: 9.53 us -> 7.84 us
    pallas_call x2, Pallas kernels: 21.5 us -> 18.4 us  [prefix_attention(): kernel_call(functools.partial(prefix_kernel, base), 9, [((256 + STAT, R),...]
    convert_element_type x1, other arithmetic: 2.48 us -> 0.01 us  [shards(): position = (PREFIX + places - first).astype(F32)]
    ppermute x37, waiting for transfers between devices: 41 us -> 43.2 us  [permute(): return lax.ppermute(value, BOTH, pairs)]
  transfers between devices with their start and end apart: 37 -> 37, of which waited for: 12 -> 12; matrix products, arithmetic and copies ran while one was open for 7% -> 6% of each run, Pallas kernels for 26% -> 25%
where the time goes in v1:
time: 149 us
  Pallas kernels  50.7 us (34%)
  waiting for transfers between devices  43.2 us (29%)
  starting transfers between devices  41.6 us (28%)
  other arithmetic  7.84 us (5%)
  local copies, waits for them, and re-layouts  4.53 us (3%)
    ppermute x37, waiting for transfers between devices, permute(): return lax.ppermute(value, BOTH, pairs)  43.2 us
    ppermute x37, starting transfers between devices, permute(): return lax.ppermute(value, BOTH, pairs)  41.6 us
    pallas_call x2, Pallas kernels, prefix_attention(): kernel_call(functools.partial(prefix_kernel, base), 9, [((256 + STAT, R),...  18.4 us
    pallas_call x2, Pallas kernels, mlp(): kernel_call(mlp_kernel, 4, [((8, rows, 256), BF16)], [pltpu.VMEM((rows, F...  13.6 us
    pallas_call x2, Pallas kernels, project(): kernel_call(functools.partial(project_kernel, base), 14, [((rows, 256), B...  9.81 us
    pallas_call x2, Pallas kernels, join(): kernel_call(functools.partial(join_kernel, base), 10, [((R, 256), BF16),...  3.51 us
    pallas_call x2, Pallas kernels, own_attention(): kernel_call(functools.partial(own_kernel, base), len(keys) + 2, [((256, r...  3.08 us
  transfers between devices with their start and end apart: 37, of which 12 were waited for; matrix products, arithmetic and copies ran while one was open for 6% of the time, Pallas kernels for 25%

profile of v1, /device:TPU:0, one launch (start us, length us, event | category | flops | bytes accessed | tf_op | source)
XLA Modules:
  0.0 148.9 jit_solution(7774358981518448326)
XLA Ops:
  1.7 2.9 %collective-permute-start = (bf16[512,256]{1,0:T(8,128)(2,1)S(1)}, bf16[512,256]{1,0:T(8,128)(2,1)S(1)}, u32[]{:S(2)}, u32[]{:S(2)}) collective-permute-start(bf16[512,256]{1,0:T(8,128)(2,1)S(1)} %slice.12.refs_0_), channel_id=1, source_target_pairs={{0,6},{1,7},{2,0},{3,1},{4,2},{5,3},{6,4},{7,5},{8,14},{9,15},{10,... | collective-permute-start | bytes 786440 | tf_op jit(solution)/shard_map/ppermute | solution.py:49
  9.7 2.6 %fusion = (f32[1024,128]{1,0:T(8,128)S(1)}, f32[1024,128]{1,0:T(8,128)S(1)}) fusion(f32[128]{0:T(128)S(1)} %compare_select_fusion.12, f32[128]{0:T(128)} %constant.136, f32[1024]{0:T(1024)S(1)} %subtract_convert_fusion), kind=kLoop, calls=%fused_computation.3 | loop fusion | flops 262144 | bytes 1053696 | tf_op jit(solution)/shard_map/mul | solution.py:477
  12.6 3.2 %collective-permute-done.refs_1_ = bf16[512,256]{1,0:T(8,128)(2,1)S(1)} collective-permute-done((bf16[512,256]{1,0:T(8,128)(2,1)S(1)}, bf16[512,256]{1,0:T(8,128)(2,1)S(1)}, u32[]{:S(2)}, u32[]{:S(2)}) %collective-permute-start) | collective-permute-done | bytes 262176 | tf_op jit(solution)/shard_map/ppermute | solution.py:49
  16.4 3.2 %collective-permute-done.2.refs_3_ = bf16[512,256]{1,0:T(8,128)(2,1)S(1)} collective-permute-done((bf16[512,256]{1,0:T(8,128)(2,1)S(1)}, bf16[512,256]{1,0:T(8,128)(2,1)S(1)}, u32[]{:S(2)}, u32[]{:S(2)}) %collective-permute-start.2) | collective-permute-done | bytes 262176 | tf_op jit(solution)/shard_map/ppermute | solution.py:49
  20.6 2.0 %collective-permute-start.8 = (bf16[512,256]{1,0:T(8,128)(2,1)S(1)}, bf16[512,256]{1,0:T(8,128)(2,1)S(1)}, u32[]{:S(2)}, u32[]{:S(2)}) collective-permute-start(bf16[512,256]{1,0:T(8,128)(2,1)S(1)} %slice.15.refs_0_), channel_id=1, source_target_pairs={{0,4},{1,5},{2,6},{3,7},{4,0},{5,1},{6,2},{7,3},{8,12},{9,13},{10,... | collective-permute-start | bytes 786440 | tf_op jit(solution)/shard_map/ppermute | solution.py:49
  22.7 1.4 collective-permute-start.7
  24.1 4.1 %collective-permute-start.17 = (bf16[1024,512]{1,0:T(8,128)(2,1)S(1)}, bf16[1024,512]{1,0:T(8,128)(2,1)S(1)}, u32[]{:S(2)}, u32[]{:S(2)}) collective-permute-start(bf16[1024,512]{1,0:T(8,128)(2,1)S(1)} %bitcast.6), channel_id=1, source_target_pairs={{0,24},{1,97},{2,26},{3,99},{4,28},{5,101},{6,30},{7,103},{8,0},{9... | collective-permute-start | bytes 3145736 | tf_op jit(solution)/shard_map/ppermute | solution.py:49
  28.2 8.0 %collective-permute-done.9.refs_3_ = bf16[512,256]{1,0:T(8,128)(2,1)S(1)} collective-permute-done((bf16[512,256]{1,0:T(8,128)(2,1)S(1)}, bf16[512,256]{1,0:T(8,128)(2,1)S(1)}, u32[]{:S(2)}, u32[]{:S(2)}) %collective-permute-start.9) | collective-permute-done | bytes 262176 | tf_op jit(solution)/shard_map/ppermute | solution.py:49
  36.1 3.9 %collective-permute-start.18 = (bf16[1024,512]{1,0:T(8,128)(2,1)S(1)}, bf16[1024,512]{1,0:T(8,128)(2,1)S(1)}, u32[]{:S(2)}, u32[]{:S(2)}) collective-permute-start(bf16[1024,512]{1,0:T(8,128)(2,1)S(1)} %bitcast.7), channel_id=1, source_target_pairs={{0,16},{1,65},{2,18},{3,67},{4,20},{5,69},{6,22},{7,71},{8,24},{9,... | collective-permute-start | bytes 3145736 | tf_op jit(solution)/shard_map/ppermute | solution.py:49
  41.0 1.9 %copy-done.1 = bf16[2048,768]{1,0:T(8,128)(2,1)S(1)} copy-done((bf16[2048,768]{1,0:T(8,128)(2,1)S(1)}, bf16[2048,768]{1,0:T(8,128)(2,1)}, u32[]{:S(2)}) %copy-start.1) | copy-done | bytes 3145752
  42.9 4.9 %shard_map.131 = (bf16[512,256]{1,0:T(8,128)(2,1)S(1)}, bf16[512,512]{1,0:T(8,128)(2,1)S(1)}, bf16[512,2048]{1,0:T(8,128)(2,1)S(1)}) custom-call(s32[8]{0:T(128)S(1)} %pad_add_fusion.2.pos.block, bf16[512,256]{1,0:T(8,128)(2,1)S(1)} %slice.12.refs_0_, bf16[512,256]{1,0:T(8,128)(2,1)S(1)} %collective-permute-done.refs_1_, ...), custom_call_target="tpu_custom_call" | custom-call | flops 1610612736 | bytes 4194304 | tf_op jit(solution)/shard_map/pallas_call | solution.py:184
  49.9 3.0 %collective-permute-start.14 = (bf16[512,256]{1,0:T(8,128)(2,1)S(1)}, bf16[512,256]{1,0:T(8,128)(2,1)S(1)}, u32[]{:S(2)}, u32[]{:S(2)}) collective-permute-start(bf16[512,256]{1,0:T(8,128)(2,1)S(1)} %get-tuple-element.70.q_ref.refs_0_), channel_id=1, source_target_pairs={{0,96},{1,25},{2,98},{3,27},{4,100},{5,29},{6,102},{7,31},{8,104},... | collective-permute-start | bytes 786440 | tf_op jit(solution)/shard_map/ppermute | solution.py:49
  52.9 1.3 collective-permute-start.15
  54.2 5.4 %collective-permute-done.14.refs_1_ = bf16[512,256]{1,0:T(8,128)(2,1)S(1)} collective-permute-done((bf16[512,256]{1,0:T(8,128)(2,1)S(1)}, bf16[512,256]{1,0:T(8,128)(2,1)S(1)}, u32[]{:S(2)}, u32[]{:S(2)}) %collective-permute-start.14) | collective-permute-done | bytes 262176 | tf_op jit(solution)/shard_map/ppermute | solution.py:49
  59.6 4.9 %shard_map.133 = (bf16[512,256]{1,0:T(8,128)(2,1)S(1)}, bf16[512,512]{1,0:T(8,128)(2,1)S(1)}, bf16[512,2048]{1,0:T(8,128)(2,1)S(1)}) custom-call(s32[8]{0:T(128)S(1)} %pad_add_fusion.2.pos.block, bf16[512,256]{1,0:T(8,128)(2,1)S(1)} %slice.15.refs_0_, bf16[512,256]{1,0:T(8,128)(2,1)S(1)} %collective-permute-done.7.refs_1_, ...), custom_call_target="tpu_custom_call" | custom-call | flops 1610612736 | bytes 4194304 | tf_op jit(solution)/shard_map/pallas_call | solution.py:184
  64.5 3.8 %collective-permute-start.20 = (bf16[512,256]{1,0:T(8,128)(2,1)S(1)}, bf16[512,256]{1,0:T(8,128)(2,1)S(1)}, u32[]{:S(2)}, u32[]{:S(2)}) collective-permute-start(bf16[512,256]{1,0:T(8,128)(2,1)S(1)} %get-tuple-element.72.q_ref.refs_0_), channel_id=1, source_target_pairs={{0,96},{1,25},{2,98},{3,27},{4,100},{5,29},{6,102},{7,31},{8,104},... | collective-permute-start | bytes 786440 | tf_op jit(solution)/shard_map/ppermute | solution.py:49
  68.2 1.6 %collective-permute-start.21 = (bf16[512,256]{1,0:T(8,128)(2,1)S(1)}, bf16[512,256]{1,0:T(8,128)(2,1)S(1)}, u32[]{:S(2)}, u32[]{:S(2)}) collective-permute-start(bf16[512,256]{1,0:T(8,128)(2,1)S(1)} %get-tuple-element.72.q_ref.refs_0_), channel_id=1, source_target_pairs={{0,64},{1,17},{2,66},{3,19},{4,68},{5,21},{6,70},{7,23},{8,72},{9,... | collective-permute-start | bytes 786440 | tf_op jit(solution)/shard_map/ppermute | solution.py:49
  71.1 1.4 shard_map.132
  72.6 1.7 %shard_map.134 = (f32[256,512]{1,0:T(8,128)S(1)}, f32[8,512]{1,0:T(8,128)S(1)}) custom-call(s32[8]{0:T(128)S(1)} %pad_add_fusion.3.starts, bf16[512,256]{1,0:T(8,128)(2,1)S(1)} %get-tuple-element.72.q_ref.refs_0_, bf16[512,512]{1,0:T(8,128)(2,1)S(1)} %get-tuple-element.99.refs_0_, bf16[512,512]{1,0:T(8,128)(2,1)S(1)} %get-tuple-element.68.refs_1_), custom_call_target="tpu_custom_call" | custom-call | flops 402653184 | bytes 4194304 | tf_op jit(solution)/shard_map/pallas_call | solution.py:271
  74.3 8.8 %shard_map.135 = (bf16[272,512]{1,0:T(8,128)(2,1)S(1)}, bf16[272,512]{1,0:T(8,128)(2,1)S(1)}, bf16[272,512]{1,0:T(8,128)(2,1)S(1)}, bf16[272,512]{1,0:T(8,128)(2,1)S(1)}) custom-call(s32[48]{0:T(128)S(1)} %reshape.84.seg, bf16[512,256]{1,0:T(8,128)(2,1)S(1)} %get-tuple-element.70.q_ref.refs_0_, bf16[512,256]{1,0:T(8,128)(2,1)S(1)} %collective-permute-done.14.refs_1_, ...), custom_call_target="tpu_custom_call" | custom-call | flops 1073741824 | bytes 4194304 | tf_op jit(solution)/shard_map/pallas_call | solution.py:361
  83.1 9.6 %shard_map.136 = (bf16[272,512]{1,0:T(8,128)(2,1)S(1)}, bf16[272,512]{1,0:T(8,128)(2,1)S(1)}, bf16[272,512]{1,0:T(8,128)(2,1)S(1)}, bf16[272,512]{1,0:T(8,128)(2,1)S(1)}) custom-call(s32[48]{0:T(128)S(1)} %reshape.84.seg, bf16[512,256]{1,0:T(8,128)(2,1)S(1)} %get-tuple-element.72.q_ref.refs_0_, bf16[512,256]{1,0:T(8,128)(2,1)S(1)} %collective-permute-done.20.refs_1_, ...), custom_call_target="tpu_custom_call" | custom-call | flops 1073741824 | bytes 4194304 | tf_op jit(solution)/shard_map/pallas_call | solution.py:361
  92.9 1.9 %collective-permute-start.25 = (bf16[272,512]{1,0:T(8,128)(2,1)S(1)}, bf16[272,512]{1,0:T(8,128)(2,1)S(1)}, u32[]{:S(2)}, u32[]{:S(2)}) collective-permute-start(bf16[272,512]{1,0:T(8,128)(2,1)S(1)} %get-tuple-element.79), channel_id=1, source_target_pairs={{0,32},{1,9},{2,34},{3,11},{4,36},{5,13},{6,38},{7,15},{8,40},{9,1... | collective-permute-start | bytes 835592 | tf_op jit(solution)/shard_map/ppermute | solution.py:49
  94.8 6.8 %shard_map.137.md_ref = bf16[8,512,256]{2,1,0:T(8,128)(2,1)S(1)} custom-call(s32[8]{0:T(128)S(1)} %pad_add_fusion.2.pos.block, bf16[512,2048]{1,0:T(8,128)(2,1)S(1)} %get-tuple-element.74.x_ref, bf16[2048,1024]{1,0:T(8,128)(2,1)S(1)} %copy-done.6, bf16[1024,2048]{1,0:T(8,128)(2,1)S(1)} %copy-done.7), custom_call_target="tpu_custom_call" | custom-call | flops 4294967296 | bytes 4194304 | tf_op jit(solution)/shard_map/pallas_call | solution.py:220
  101.7 2.2 %collective-permute-done.25.b3 = bf16[272,512]{1,0:T(8,128)(2,1)S(1)} collective-permute-done((bf16[272,512]{1,0:T(8,128)(2,1)S(1)}, bf16[272,512]{1,0:T(8,128)(2,1)S(1)}, u32[]{:S(2)}, u32[]{:S(2)}) %collective-permute-start.25) | collective-permute-done | bytes 278560 | tf_op jit(solution)/shard_map/ppermute | solution.py:49
  103.9 1.8 %shard_map.138 = (bf16[512,256]{1,0:T(8,128)(2,1)S(1)}, bf16[4,512,256]{2,1,0:T(8,128)(2,1)S(1)}) custom-call(s32[8]{0:T(128)S(1)} %pad_add_fusion.2.pos.block, s32[8]{0:T(128)S(1)} %pad_add_fusion.3.starts, f32[256,512]{1,0:T(8,128)S(1)} %get-tuple-element.75.numer_ref, f32[8,512]{1,0:T(8,128)S(1)} %get-tuple-element.76.stat_ref, ...), custom_call_target="tpu_custom_call" | custom-call | flops 268435456 | bytes 4194304 | tf_op jit(solution)/shard_map/pallas_call | solution.py:408
  106.0 1.5 %collective-permute-start.30 = (bf16[272,512]{1,0:T(8,128)(2,1)S(1)}, bf16[272,512]{1,0:T(8,128)(2,1)S(1)}, u32[]{:S(2)}, u32[]{:S(2)}) collective-permute-start(bf16[272,512]{1,0:T(8,128)(2,1)S(1)} %get-tuple-element.90), channel_id=1, source_target_pairs={{0,96},{1,25},{2,98},{3,27},{4,100},{5,29},{6,102},{7,31},{8,104},... | collective-permute-start | bytes 835592 | tf_op jit(solution)/shard_map/ppermute | solution.py:49
  109.4 6.8 %shard_map.140.md_ref = bf16[8,512,256]{2,1,0:T(8,128)(2,1)S(1)} custom-call(s32[8]{0:T(128)S(1)} %pad_add_fusion.2.pos.block, bf16[512,2048]{1,0:T(8,128)(2,1)S(1)} %get-tuple-element.87.x_ref, bf16[2048,1024]{1,0:T(8,128)(2,1)S(1)} %copy-done.6, bf16[1024,2048]{1,0:T(8,128)(2,1)S(1)} %copy-done.7), custom_call_target="tpu_custom_call" | custom-call | flops 4294967296 | bytes 4194304 | tf_op jit(solution)/shard_map/pallas_call | solution.py:220
  118.6 1.8 %shard_map.141 = (bf16[512,256]{1,0:T(8,128)(2,1)S(1)}, bf16[4,512,256]{2,1,0:T(8,128)(2,1)S(1)}) custom-call(s32[8]{0:T(128)S(1)} %pad_add_fusion.2.pos.block, s32[8]{0:T(128)S(1)} %pad_add_fusion.3.starts, f32[256,512]{1,0:T(8,128)S(1)} %get-tuple-element.88.numer_ref, f32[8,512]{1,0:T(8,128)S(1)} %get-tuple-element.89.stat_ref, ...), custom_call_target="tpu_custom_call" | custom-call | flops 268435456 | bytes 4194304 | tf_op jit(solution)/shard_map/pallas_call | solution.py:408
  121.6 2.2 %collective-permute-start.29 = (bf16[512,256]{1,0:T(8,128)(2,1)S(1)}, bf16[512,256]{1,0:T(8,128)(2,1)S(1)}, u32[]{:S(2)}, u32[]{:S(2)}) collective-permute-start(bf16[512,256]{1,0:T(8,128)(2,1)S(1)} %get-tuple-element.85), channel_id=1, source_target_pairs={{0,6},{1,7},{2,0},{3,1},{4,2},{5,3},{6,4},{7,5},{8,14},{9,15},{10,... | collective-permute-start | bytes 786440 | tf_op jit(solution)/shard_map/ppermute | solution.py:49
  125.8 2.1 %collective-permute-start.35 = (bf16[512,256]{1,0:T(8,128)(2,1)S(1)}, bf16[512,256]{1,0:T(8,128)(2,1)S(1)}, u32[]{:S(2)}, u32[]{:S(2)}) collective-permute-start(bf16[512,256]{1,0:T(8,128)(2,1)S(1)} %get-tuple-element.97), channel_id=1, source_target_pairs={{0,4},{1,5},{2,6},{3,7},{4,0},{5,1},{6,2},{7,3},{8,12},{9,13},{10,... | collective-permute-start | bytes 786440 | tf_op jit(solution)/shard_map/ppermute | solution.py:49
  128.0 8.6 %collective-permute-done.27 = bf16[512,256]{1,0:T(8,128)(2,1)S(1)} collective-permute-done((bf16[512,256]{1,0:T(8,128)(2,1)S(1)}, bf16[512,256]{1,0:T(8,128)(2,1)S(1)}, u32[]{:S(2)}, u32[]{:S(2)}) %collective-permute-start.27) | collective-permute-done | bytes 262176 | tf_op jit(solution)/shard_map/ppermute | solution.py:49
  138.7 8.6 %collective-permute-done.34 = bf16[512,256]{1,0:T(8,128)(2,1)S(1)} collective-permute-done((bf16[512,256]{1,0:T(8,128)(2,1)S(1)}, bf16[512,256]{1,0:T(8,128)(2,1)S(1)}, u32[]{:S(2)}, u32[]{:S(2)}) %collective-permute-start.34) | collective-permute-done | bytes 262176 | tf_op jit(solution)/shard_map/ppermute | solution.py:49
  (100 shorter events, 24.0 us)
Async XLA Ops:
  1.7 14.1 %collective-permute-start = (bf16[512,256]{1,0:T(8,128)(2,1)S(1)}, bf16[512,256]{1,0:T(8,128)(2,1)S(1)}, u32[]{:S(2)}, u32[]{:S(2)}) collective-permute-start(bf16[512,256]{1,0:T(8,128)(2,1)S(1)} %slice.12.refs_0_), channel_id=1, source_target_pairs={{0,6},{1,7},{2,0},{3,1},{4,2},{5,3},{6,4},{7,5},{8,14},{9,15},{10,... | collective-permute-start | bytes 786440 | tf_op jit(solution)/shard_map/ppermute | solution.py:49
  4.7 11.2 %collective-permute-start.1 = (bf16[512,256]{1,0:T(8,128)(2,1)S(1)}, bf16[512,256]{1,0:T(8,128)(2,1)S(1)}, u32[]{:S(2)}, u32[]{:S(2)}) collective-permute-start(bf16[512,256]{1,0:T(8,128)(2,1)S(1)} %slice.12.refs_0_), channel_id=1, source_target_pairs={{0,4},{1,5},{2,6},{3,7},{4,0},{5,1},{6,2},{7,3},{8,12},{9,13},{10,... | collective-permute-start | bytes 786440 | tf_op jit(solution)/shard_map/ppermute | solution.py:49
  5.5 14.1 %collective-permute-start.2 = (bf16[512,256]{1,0:T(8,128)(2,1)S(1)}, bf16[512,256]{1,0:T(8,128)(2,1)S(1)}, u32[]{:S(2)}, u32[]{:S(2)}) collective-permute-start(bf16[512,256]{1,0:T(8,128)(2,1)S(1)} %slice.12.refs_0_), channel_id=1, source_target_pairs={{0,2},{1,3},{2,4},{3,5},{4,6},{5,7},{6,0},{7,1},{8,10},{9,11},{10,... | collective-permute-start | bytes 786440 | tf_op jit(solution)/shard_map/ppermute | solution.py:49
  6.3 14.3 %collective-permute-start.3 = (bf16[512,256]{1,0:T(8,128)(2,1)S(1)}, bf16[512,256]{1,0:T(8,128)(2,1)S(1)}, u32[]{:S(2)}, u32[]{:S(2)}) collective-permute-start(bf16[512,256]{1,0:T(8,128)(2,1)S(1)} %slice.12.refs_0_), channel_id=1, source_target_pairs={{0,1},{1,0},{2,3},{3,2},{4,5},{5,4},{6,7},{7,6},{8,9},{9,8},{10,11... | collective-permute-start | bytes 786440 | tf_op jit(solution)/shard_map/ppermute | solution.py:49
  15.8 6.8 %collective-permute-start.4 = (bf16[512,256]{1,0:T(8,128)(2,1)S(1)}, bf16[512,256]{1,0:T(8,128)(2,1)S(1)}, u32[]{:S(2)}, u32[]{:S(2)}) collective-permute-start(bf16[512,256]{1,0:T(8,128)(2,1)S(1)} %collective-permute-done.refs_1_), channel_id=1, source_target_pairs={{0,1},{1,0},{2,3},{3,2},{4,5},{5,4},{6,7},{7,6},{8,9},{9,8},{10,11... | collective-permute-start | bytes 786440 | tf_op jit(solution)/shard_map/ppermute | solution.py:49
  15.8 8.2 %collective-permute-start.5 = (bf16[512,256]{1,0:T(8,128)(2,1)S(1)}, bf16[512,256]{1,0:T(8,128)(2,1)S(1)}, u32[]{:S(2)}, u32[]{:S(2)}) collective-permute-start(bf16[512,256]{1,0:T(8,128)(2,1)S(1)} %collective-permute-done.1.refs_2_), channel_id=1, source_target_pairs={{0,1},{1,0},{2,3},{3,2},{4,5},{5,4},{6,7},{7,6},{8,9},{9,8},{10,11... | collective-permute-start | bytes 786440 | tf_op jit(solution)/shard_map/ppermute | solution.py:49
  20.5 15.6 %collective-permute-start.9 = (bf16[512,256]{1,0:T(8,128)(2,1)S(1)}, bf16[512,256]{1,0:T(8,128)(2,1)S(1)}, u32[]{:S(2)}, u32[]{:S(2)}) collective-permute-start(bf16[512,256]{1,0:T(8,128)(2,1)S(1)} %slice.15.refs_0_), channel_id=1, source_target_pairs={{0,2},{1,3},{2,4},{3,5},{4,6},{5,7},{6,0},{7,1},{8,10},{9,11},{10,... | collective-permute-start | bytes 786440 | tf_op jit(solution)/shard_map/ppermute | solution.py:49
  20.6 19.4 %collective-permute-start.8 = (bf16[512,256]{1,0:T(8,128)(2,1)S(1)}, bf16[512,256]{1,0:T(8,128)(2,1)S(1)}, u32[]{:S(2)}, u32[]{:S(2)}) collective-permute-start(bf16[512,256]{1,0:T(8,128)(2,1)S(1)} %slice.15.refs_0_), channel_id=1, source_target_pairs={{0,4},{1,5},{2,6},{3,7},{4,0},{5,1},{6,2},{7,3},{8,12},{9,13},{10,... | collective-permute-start | bytes 786440 | tf_op jit(solution)/shard_map/ppermute | solution.py:49
  22.7 25.2 %collective-permute-start.7 = (bf16[512,256]{1,0:T(8,128)(2,1)S(1)}, bf16[512,256]{1,0:T(8,128)(2,1)S(1)}, u32[]{:S(2)}, u32[]{:S(2)}) collective-permute-start(bf16[512,256]{1,0:T(8,128)(2,1)S(1)} %slice.15.refs_0_), channel_id=1, source_target_pairs={{0,6},{1,7},{2,0},{3,1},{4,2},{5,3},{6,4},{7,5},{8,14},{9,15},{10,... | collective-permute-start | bytes 786440 | tf_op jit(solution)/shard_map/ppermute | solution.py:49
  24.0 23.9 %collective-permute-start.10 = (bf16[512,256]{1,0:T(8,128)(2,1)S(1)}, bf16[512,256]{1,0:T(8,128)(2,1)S(1)}, u32[]{:S(2)}, u32[]{:S(2)}) collective-permute-start(bf16[512,256]{1,0:T(8,128)(2,1)S(1)} %slice.15.refs_0_), channel_id=1, source_target_pairs={{0,1},{1,0},{2,3},{3,2},{4,5},{5,4},{6,7},{7,6},{8,9},{9,8},{10,11... | collective-permute-start | bytes 786440 | tf_op jit(solution)/shard_map/ppermute | solution.py:49
  24.1 45.8 %collective-permute-start.17 = (bf16[1024,512]{1,0:T(8,128)(2,1)S(1)}, bf16[1024,512]{1,0:T(8,128)(2,1)S(1)}, u32[]{:S(2)}, u32[]{:S(2)}) collective-permute-start(bf16[1024,512]{1,0:T(8,128)(2,1)S(1)} %bitcast.6), channel_id=1, source_target_pairs={{0,24},{1,97},{2,26},{3,99},{4,28},{5,101},{6,30},{7,103},{8,0},{9... | collective-permute-start | bytes 3145736 | tf_op jit(solution)/shard_map/ppermute | solution.py:49
  36.1 38.1 %collective-permute-start.18 = (bf16[1024,512]{1,0:T(8,128)(2,1)S(1)}, bf16[1024,512]{1,0:T(8,128)(2,1)S(1)}, u32[]{:S(2)}, u32[]{:S(2)}) collective-permute-start(bf16[1024,512]{1,0:T(8,128)(2,1)S(1)} %bitcast.7), channel_id=1, source_target_pairs={{0,16},{1,65},{2,18},{3,67},{4,20},{5,69},{6,22},{7,71},{8,24},{9,... | collective-permute-start | bytes 3145736 | tf_op jit(solution)/shard_map/ppermute | solution.py:49
  40.0 34.2 %collective-permute-start.19 = (bf16[1024,512]{1,0:T(8,128)(2,1)S(1)}, bf16[1024,512]{1,0:T(8,128)(2,1)S(1)}, u32[]{:S(2)}, u32[]{:S(2)}) collective-permute-start(bf16[1024,512]{1,0:T(8,128)(2,1)S(1)} %bitcast.8), channel_id=1, source_target_pairs={{0,8},{1,33},{2,10},{3,35},{4,12},{5,37},{6,14},{7,39},{8,16},{9,4... | collective-permute-start | bytes 3145736 | tf_op jit(solution)/shard_map/ppermute | solution.py:49
  49.9 9.7 %collective-permute-start.14 = (bf16[512,256]{1,0:T(8,128)(2,1)S(1)}, bf16[512,256]{1,0:T(8,128)(2,1)S(1)}, u32[]{:S(2)}, u32[]{:S(2)}) collective-permute-start(bf16[512,256]{1,0:T(8,128)(2,1)S(1)} %get-tuple-element.70.q_ref.refs_0_), channel_id=1, source_target_pairs={{0,96},{1,25},{2,98},{3,27},{4,100},{5,29},{6,102},{7,31},{8,104},... | collective-permute-start | bytes 786440 | tf_op jit(solution)/shard_map/ppermute | solution.py:49
  52.9 11.6 %collective-permute-start.15 = (bf16[512,256]{1,0:T(8,128)(2,1)S(1)}, bf16[512,256]{1,0:T(8,128)(2,1)S(1)}, u32[]{:S(2)}, u32[]{:S(2)}) collective-permute-start(bf16[512,256]{1,0:T(8,128)(2,1)S(1)} %get-tuple-element.70.q_ref.refs_0_), channel_id=1, source_target_pairs={{0,64},{1,17},{2,66},{3,19},{4,68},{5,21},{6,70},{7,23},{8,72},{9,... | collective-permute-start | bytes 786440 | tf_op jit(solution)/shard_map/ppermute | solution.py:49
  59.6 8.7 %collective-permute-start.16 = (bf16[512,256]{1,0:T(8,128)(2,1)S(1)}, bf16[512,256]{1,0:T(8,128)(2,1)S(1)}, u32[]{:S(2)}, u32[]{:S(2)}) collective-permute-start(bf16[512,256]{1,0:T(8,128)(2,1)S(1)} %get-tuple-element.70.q_ref.refs_0_), channel_id=1, source_target_pairs={{0,32},{1,9},{2,34},{3,11},{4,36},{5,13},{6,38},{7,15},{8,40},{9,1... | collective-permute-start | bytes 786440 | tf_op jit(solution)/shard_map/ppermute | solution.py:49
  64.5 18.6 %collective-permute-start.20 = (bf16[512,256]{1,0:T(8,128)(2,1)S(1)}, bf16[512,256]{1,0:T(8,128)(2,1)S(1)}, u32[]{:S(2)}, u32[]{:S(2)}) collective-permute-start(bf16[512,256]{1,0:T(8,128)(2,1)S(1)} %get-tuple-element.72.q_ref.refs_0_), channel_id=1, source_target_pairs={{0,96},{1,25},{2,98},{3,27},{4,100},{5,29},{6,102},{7,31},{8,104},... | collective-permute-start | bytes 786440 | tf_op jit(solution)/shard_map/ppermute | solution.py:49
  68.2 14.8 %collective-permute-start.21 = (bf16[512,256]{1,0:T(8,128)(2,1)S(1)}, bf16[512,256]{1,0:T(8,128)(2,1)S(1)}, u32[]{:S(2)}, u32[]{:S(2)}) collective-permute-start(bf16[512,256]{1,0:T(8,128)(2,1)S(1)} %get-tuple-element.72.q_ref.refs_0_), channel_id=1, source_target_pairs={{0,64},{1,17},{2,66},{3,19},{4,68},{5,21},{6,70},{7,23},{8,72},{9,... | collective-permute-start | bytes 786440 | tf_op jit(solution)/shard_map/ppermute | solution.py:49
  69.8 13.3 %collective-permute-start.22 = (bf16[512,256]{1,0:T(8,128)(2,1)S(1)}, bf16[512,256]{1,0:T(8,128)(2,1)S(1)}, u32[]{:S(2)}, u32[]{:S(2)}) collective-permute-start(bf16[512,256]{1,0:T(8,128)(2,1)S(1)} %get-tuple-element.72.q_ref.refs_0_), channel_id=1, source_target_pairs={{0,32},{1,9},{2,34},{3,11},{4,36},{5,13},{6,38},{7,15},{8,40},{9,1... | collective-permute-start | bytes 786440 | tf_op jit(solution)/shard_map/ppermute | solution.py:49
  92.7 8.9 %collective-permute-start.23 = (bf16[272,512]{1,0:T(8,128)(2,1)S(1)}, bf16[272,512]{1,0:T(8,128)(2,1)S(1)}, u32[]{:S(2)}, u32[]{:S(2)}) collective-permute-start(bf16[272,512]{1,0:T(8,128)(2,1)S(1)} %get-tuple-element.77), channel_id=1, source_target_pairs={{0,96},{1,25},{2,98},{3,27},{4,100},{5,29},{6,102},{7,31},{8,104},... | collective-permute-start | bytes 835592 | tf_op jit(solution)/shard_map/ppermute | solution.py:49
  92.8 8.9 %collective-permute-start.24 = (bf16[272,512]{1,0:T(8,128)(2,1)S(1)}, bf16[272,512]{1,0:T(8,128)(2,1)S(1)}, u32[]{:S(2)}, u32[]{:S(2)}) collective-permute-start(bf16[272,512]{1,0:T(8,128)(2,1)S(1)} %get-tuple-element.78), channel_id=1, source_target_pairs={{0,64},{1,17},{2,66},{3,19},{4,68},{5,21},{6,70},{7,23},{8,72},{9,... | collective-permute-start | bytes 835592 | tf_op jit(solution)/shard_map/ppermute | solution.py:49
  92.9 11.0 %collective-permute-start.25 = (bf16[272,512]{1,0:T(8,128)(2,1)S(1)}, bf16[272,512]{1,0:T(8,128)(2,1)S(1)}, u32[]{:S(2)}, u32[]{:S(2)}) collective-permute-start(bf16[272,512]{1,0:T(8,128)(2,1)S(1)} %get-tuple-element.79), channel_id=1, source_target_pairs={{0,32},{1,9},{2,34},{3,11},{4,36},{5,13},{6,38},{7,15},{8,40},{9,1... | collective-permute-start | bytes 835592 | tf_op jit(solution)/shard_map/ppermute | solution.py:49
  105.7 10.5 %collective-permute-start.26 = (bf16[4,512,256]{2,1,0:T(8,128)(2,1)S(1)}, bf16[4,512,256]{2,1,0:T(8,128)(2,1)S(1)}, u32[]{:S(2)}, u32[]{:S(2)}) collective-permute-start(bf16[4,512,256]{2,1,0:T(8,128)(2,1)S(1)} %get-tuple-element.81), channel_id=1, source_target_pairs={{0,1},{1,0},{2,3},{3,2},{4,5},{5,4},{6,7},{7,6},{8,9},{9,8},{10,11... | collective-permute-start | bytes 3145736 | tf_op jit(solution)/shard_map/ppermute | solution.py:49
  106.0 11.3 %collective-permute-start.30 = (bf16[272,512]{1,0:T(8,128)(2,1)S(1)}, bf16[272,512]{1,0:T(8,128)(2,1)S(1)}, u32[]{:S(2)}, u32[]{:S(2)}) collective-permute-start(bf16[272,512]{1,0:T(8,128)(2,1)S(1)} %get-tuple-element.90), channel_id=1, source_target_pairs={{0,96},{1,25},{2,98},{3,27},{4,100},{5,29},{6,102},{7,31},{8,104},... | collective-permute-start | bytes 835592 | tf_op jit(solution)/shard_map/ppermute | solution.py:49
  107.6 9.8 %collective-permute-start.31 = (bf16[272,512]{1,0:T(8,128)(2,1)S(1)}, bf16[272,512]{1,0:T(8,128)(2,1)S(1)}, u32[]{:S(2)}, u32[]{:S(2)}) collective-permute-start(bf16[272,512]{1,0:T(8,128)(2,1)S(1)} %get-tuple-element.91), channel_id=1, source_target_pairs={{0,64},{1,17},{2,66},{3,19},{4,68},{5,21},{6,70},{7,23},{8,72},{9,... | collective-permute-start | bytes 835592 | tf_op jit(solution)/shard_map/ppermute | solution.py:49
  108.1 10.5 %collective-permute-start.32 = (bf16[272,512]{1,0:T(8,128)(2,1)S(1)}, bf16[272,512]{1,0:T(8,128)(2,1)S(1)}, u32[]{:S(2)}, u32[]{:S(2)}) collective-permute-start(bf16[272,512]{1,0:T(8,128)(2,1)S(1)} %get-tuple-element.92), channel_id=1, source_target_pairs={{0,32},{1,9},{2,34},{3,11},{4,36},{5,13},{6,38},{7,15},{8,40},{9,1... | collective-permute-start | bytes 835592 | tf_op jit(solution)/shard_map/ppermute | solution.py:49
  120.5 16.1 %collective-permute-start.27 = (bf16[512,256]{1,0:T(8,128)(2,1)S(1)}, bf16[512,256]{1,0:T(8,128)(2,1)S(1)}, u32[]{:S(2)}, u32[]{:S(2)}) collective-permute-start(bf16[512,256]{1,0:T(8,128)(2,1)S(1)} %get-tuple-element.83), channel_id=1, source_target_pairs={{0,2},{1,3},{2,4},{3,5},{4,6},{5,7},{6,0},{7,1},{8,10},{9,11},{10,... | collective-permute-start | bytes 786440 | tf_op jit(solution)/shard_map/ppermute | solution.py:49
  120.5 16.0 %collective-permute-start.28 = (bf16[512,256]{1,0:T(8,128)(2,1)S(1)}, bf16[512,256]{1,0:T(8,128)(2,1)S(1)}, u32[]{:S(2)}, u32[]{:S(2)}) collective-permute-start(bf16[512,256]{1,0:T(8,128)(2,1)S(1)} %get-tuple-element.84), channel_id=1, source_target_pairs={{0,4},{1,5},{2,6},{3,7},{4,0},{5,1},{6,2},{7,3},{8,12},{9,13},{10,... | collective-permute-start | bytes 786440 | tf_op jit(solution)/shard_map/ppermute | solution.py:49
  121.6 15.9 %collective-permute-start.29 = (bf16[512,256]{1,0:T(8,128)(2,1)S(1)}, bf16[512,256]{1,0:T(8,128)(2,1)S(1)}, u32[]{:S(2)}, u32[]{:S(2)}) collective-permute-start(bf16[512,256]{1,0:T(8,128)(2,1)S(1)} %get-tuple-element.85), channel_id=1, source_target_pairs={{0,6},{1,7},{2,0},{3,1},{4,2},{5,3},{6,4},{7,5},{8,14},{9,15},{10,... | collective-permute-start | bytes 786440 | tf_op jit(solution)/shard_map/ppermute | solution.py:49
  124.9 22.3 %collective-permute-start.34 = (bf16[512,256]{1,0:T(8,128)(2,1)S(1)}, bf16[512,256]{1,0:T(8,128)(2,1)S(1)}, u32[]{:S(2)}, u32[]{:S(2)}) collective-permute-start(bf16[512,256]{1,0:T(8,128)(2,1)S(1)} %get-tuple-element.96), channel_id=1, source_target_pairs={{0,2},{1,3},{2,4},{3,5},{4,6},{5,7},{6,0},{7,1},{8,10},{9,11},{10,... | collective-permute-start | bytes 786440 | tf_op jit(solution)/shard_map/ppermute | solution.py:49
  125.8 21.4 %collective-permute-start.35 = (bf16[512,256]{1,0:T(8,128)(2,1)S(1)}, bf16[512,256]{1,0:T(8,128)(2,1)S(1)}, u32[]{:S(2)}, u32[]{:S(2)}) collective-permute-start(bf16[512,256]{1,0:T(8,128)(2,1)S(1)} %get-tuple-element.97), channel_id=1, source_target_pairs={{0,4},{1,5},{2,6},{3,7},{4,0},{5,1},{6,2},{7,3},{8,12},{9,13},{10,... | collective-permute-start | bytes 786440 | tf_op jit(solution)/shard_map/ppermute | solution.py:49
  136.5 11.4 %collective-permute-start.36 = (bf16[512,256]{1,0:T(8,128)(2,1)S(1)}, bf16[512,256]{1,0:T(8,128)(2,1)S(1)}, u32[]{:S(2)}, u32[]{:S(2)}) collective-permute-start(bf16[512,256]{1,0:T(8,128)(2,1)S(1)} %get-tuple-element.98), channel_id=1, source_target_pairs={{0,6},{1,7},{2,0},{3,1},{4,2},{5,3},{6,4},{7,5},{8,14},{9,15},{10,... | collective-permute-start | bytes 786440 | tf_op jit(solution)/shard_map/ppermute | solution.py:49
  (14 other events, 194.6 us)
